TPU v7x, 1024 devices: a whole 4x8x16 slice. The times are simulated.
1024 devices in a mesh: seq: 64 (over z, x), head: 8 (over y), pair: 2 (over core).
Axes of the slice: x: 4, y: 8, z: 16, core: 2. Of those that a mesh axis runs over, the one named last changes fastest.
Arguments:
- query_rows: bfloat16 [8192, 2048], P('seq', ('head', 'pair')), may hold values from -6 to 6
- all_head_keys: bfloat16 [8192, 2048], P('seq', ('head', 'pair')), may hold values from -6 to 6
- value_rows: bfloat16 [8192, 2048], P('seq', ('head', 'pair')), may hold values from -6 to 6
- stream: bfloat16 [8192, 2048], P(('seq', 'head', 'pair')), may hold values from -6 to 6
- attn_gain: float32 [2048], P(('head', 'pair')), may hold values from 0.5 to 2
- out_weight: bfloat16 [2048, 2048], P(('head', 'pair')), may hold values from -0.125 to 0.125
- moe_gain: float32 [2048], replicated, may hold values from 0.5 to 2
- routes: int32 [8192, 8], P(('seq', 'head')), may hold values from 0 to 127, all different within a row; in each aligned block of 8 rows (0 to 7, 8 to 15, ...) at most 2 rows name the same one
- gate_weights: float32 [8192, 8], P(('seq', 'head')), may hold values from 0.1 to 0.4
- w_gate: bfloat16 [128, 2048, 768], P('seq', None, 'pair'), may hold values from -0.125 to 0.125
- w_up: bfloat16 [128, 2048, 768], P('seq', None, 'pair'), may hold values from -0.125 to 0.125
- w_down: bfloat16 [128, 768, 2048], P('seq', 'pair'), may hold values from -0.21875 to 0.21875
Outputs:
- layer_out: bfloat16 [8192, 2048], P(('seq', 'head', 'pair'))
Inputs may be any that keep to these rules, and one draw needn't show every extreme that they name: `routes`: each row names 8 different experts; within each aligned block of 8 rows no expert is named more than 2 times.
All inputs are finite; a program needn't handle non-finite values.
Results may differ from a plain program's by a relative error of at most 0.018.
Values may be sent and summed in bfloat16 or wider, within the bound.
No kernel may reach another device: no remote copies, remote signals or barrier semaphores. Data moves between devices by JAX's collectives and lax.ppermute only.
A program may use at most 64 MiB of HBM per device.

v0:
```python
import jax
import jax.numpy as jnp
from jax import lax
from jax.sharding import Mesh
from jax.sharding import PartitionSpec as P

HEAD_DIM = 128
SEQ = ("seq_0", "seq_1")
SEQ_HEAD_PAIR = ("seq_0", "seq_1", "head", "pair")
SEQ_HEAD = ("seq_0", "seq_1", "head")


EPSILON = 1e-06


def filled_with(shard, identity):
    return jnp.broadcast_to(jnp.asarray(identity, shard.dtype), shard.shape)


def entering(shard, axes, combine, identity):
    before = start = filled_with(shard, identity)
    total = shard
    for axis in reversed(axes):
        size, here = (lax.axis_size(axis), lax.axis_index(axis))
        pieces = lax.all_gather(total.astype(jnp.bfloat16), axis)
        inside, total = (start, start)
        for k in range(size):
            passed = k < here
            total = combine(total, pieces[k].astype(shard.dtype))
            inside = jnp.where(passed, total, inside)
        before = combine(inside, before)
    return before


def split_up(shard, dim, size):
    before, after = (shard.shape[:dim], shard.shape[dim + 1 :])
    return jnp.moveaxis(shard.reshape(*before, size, -1, *after), dim, 0)


def sent_and_summed(shard, axis, dim):
    size = lax.axis_size(axis)
    blocks = lax.all_to_all(split_up(shard, dim, size), axis, 0, 0, tiled=True)
    return jnp.sum(blocks.astype(jnp.float32), axis=0)


def joined_along(blocks, dim):
    shape = list(blocks.shape[1:])
    shape[dim] *= blocks.shape[0]
    return jnp.moveaxis(blocks, 0, dim).reshape(shape)


def sent_to_all(shard, axis):
    size = lax.axis_size(axis)
    return lax.all_to_all(
        jnp.broadcast_to(shard[None], (size, *shard.shape)), axis, 0, 0, tiled=True
    )


def collect(shard, axis, dim):
    return joined_along(sent_to_all(shard, axis), dim)


def rms_scale(values, gain_vec):
    mean_sq = jnp.mean(values * values, axis=-1, keepdims=True)
    return values * lax.rsqrt(mean_sq + EPSILON) * gain_vec


def slot_ranks(expert_ids, num_experts):
    flat_ids = expert_ids.reshape(-1)
    one_hot = (flat_ids[:, None] == jnp.arange(num_experts, dtype=jnp.int32)[None, :]).astype(
        jnp.int32
    )
    before = jnp.cumsum(one_hot, axis=0) - one_hot
    return jnp.sum(before * one_hot, axis=1)


def slot_dest(expert_ids, num_experts, capacity):
    return expert_ids.reshape(-1) * capacity + slot_ranks(expert_ids, num_experts)


def build_outgoing(block_input, expert_ids, num_experts, capacity):
    top_count = expert_ids.shape[1]
    destination = slot_dest(expert_ids, num_experts, capacity)
    slot_count = num_experts * capacity
    one_hot = (jnp.arange(slot_count, dtype=jnp.int32)[:, None] == destination[None, :]).astype(
        jnp.int32
    )
    slot_table = (
        one_hot.reshape(slot_count, block_input.shape[0], top_count)
        .sum(axis=2)
        .astype(jnp.bfloat16)
    )
    return jnp.dot(slot_table, block_input, preferred_element_type=jnp.float32).astype(jnp.bfloat16)


def add_states(earlier, later):
    return earlier + later


def body(
    query_rows,
    all_head_keys,
    value_rows,
    stream,
    attn_gain,
    out_weight,
    moe_gain,
    routes,
    gate_weights,
    w_gate,
    w_up,
    w_down,
):
    length, width_attn = query_rows.shape
    head_count = width_attn // HEAD_DIM

    def split_heads(matrix):
        return matrix.reshape(length, head_count, HEAD_DIM).transpose(1, 0, 2)

    query_head_total = split_heads(query_rows)
    key_head_total = split_heads(all_head_keys)
    value_head_total = split_heads(value_rows)
    local_state = jnp.einsum(
        "fqz,fqd->fzd", key_head_total, value_head_total, preferred_element_type=jnp.float32
    )
    previous_state = entering(local_state, SEQ, add_states, jnp.zeros_like(local_state))
    causal = (jnp.arange(length)[:, None] >= jnp.arange(length)[None, :]).astype(jnp.float32)
    scores = (
        jnp.einsum(
            "htk,hsk->hts", query_head_total, key_head_total, preferred_element_type=jnp.float32
        )
        * causal
    )
    mixed = jnp.einsum("hts,hsv->htv", scores, value_head_total.astype(jnp.float32))
    mixed = mixed + jnp.einsum("dbx,dxa->dba", query_head_total.astype(jnp.float32), previous_state)
    normed = rms_scale(mixed, attn_gain.reshape(head_count, 1, HEAD_DIM))
    attn_normed = normed.transpose(1, 0, 2).reshape(length, width_attn).astype(jnp.bfloat16)
    block_row_span = stream.shape[0]
    model_width = stream.shape[1]
    row_piece = attn_normed
    projected = sent_and_summed(
        jnp.dot(row_piece, out_weight, preferred_element_type=jnp.float32).astype(jnp.bfloat16),
        ("head", "pair"),
        0,
    )
    residual = stream.astype(jnp.float32) + projected
    moe_input = rms_scale(residual, moe_gain).astype(jnp.bfloat16)
    top_count = routes.shape[1]
    experts_here = w_gate.shape[0]
    num_experts = experts_here * lax.axis_size(SEQ)
    capacity = min(
        block_row_span, 2 * ((block_row_span * top_count + num_experts - 1) // num_experts)
    )
    my_core = lax.axis_index("pair")
    my_routes = lax.dynamic_slice_in_dim(routes, my_core * block_row_span, block_row_span, 0)
    my_weights = lax.dynamic_slice_in_dim(gate_weights, my_core * block_row_span, block_row_span, 0)
    my_dest = slot_dest(my_routes, num_experts, capacity)
    own_buffer = build_outgoing(moe_input, my_routes, num_experts, capacity)[None]
    arrived = lax.all_to_all(own_buffer, SEQ, split_axis=1, concat_axis=1, tiled=True)
    received = collect(arrived, "pair", 0)
    buffer = received.reshape(-1, model_width)
    per_block = experts_here * capacity
    out_rows = received.shape[1]
    slice_width = capacity * model_width
    row_piece = buffer
    groups = out_rows * lax.axis_size("pair") // per_block
    grouped = row_piece.reshape(groups, per_block * model_width)
    results = []
    for expert_index in range(experts_here):
        expert_rows = grouped[
            :, expert_index * slice_width : (expert_index + 1) * slice_width
        ].reshape(groups * capacity, model_width)
        gate_part = jnp.dot(expert_rows, w_gate[expert_index], preferred_element_type=jnp.float32)
        up_part = jnp.dot(expert_rows, w_up[expert_index], preferred_element_type=jnp.float32)
        activated = (jax.nn.silu(gate_part) * up_part).astype(jnp.bfloat16)
        result = jnp.dot(activated, w_down[expert_index], preferred_element_type=jnp.float32)
        results.append(result.reshape(groups, slice_width))
    expert_out = sent_and_summed(
        jnp.concatenate(results, axis=1)
        .reshape(out_rows * lax.axis_size("pair"), model_width)
        .astype(jnp.bfloat16),
        "pair",
        0,
    ).astype(jnp.bfloat16)
    returned = lax.all_to_all(expert_out, SEQ, split_axis=0, concat_axis=0, tiled=True)
    picked = (
        jnp.take(returned, my_dest, axis=0)
        .reshape(block_row_span, top_count, model_width)
        .astype(jnp.float32)
    )
    combined = jnp.einsum("rk,rkd->rd", my_weights, picked)
    return (residual + combined).astype(jnp.bfloat16)


def solution(mesh):
    split = Mesh(
        mesh.devices.reshape(16, 4, mesh.shape["head"], mesh.shape["pair"]),
        ("seq_0", "seq_1", "head", "pair"),
    )
    placed = (
        P(SEQ, ("head", "pair")),
        P(SEQ, ("head", "pair")),
        P(SEQ, ("head", "pair")),
        P(SEQ_HEAD_PAIR, None),
        P(("head", "pair")),
        P(("head", "pair"), None),
        P(),
        P(SEQ_HEAD, None),
        P(SEQ_HEAD, None),
        P(SEQ, None, "pair"),
        P(SEQ, None, "pair"),
        P(SEQ, "pair", None),
    )
    return jax.shard_map(
        body, mesh=split, in_specs=placed, out_specs=P(SEQ_HEAD_PAIR, None), check_vma=False
    )
```

profile of v0, /device:TPU:7, one launch (start us, length us, event | category | flops | bytes accessed | tf_op | source)
XLA Modules:
  0.0 270.7 jit_solution(16815218306785954993)
XLA Ops:
  0.0 1.0 convolution_convert_fusion.4
  1.0 9.1 %all-gather = bf16[512,128]{1,0:T(8,128)(2,1)S(1)} all-gather(bf16[128,128]{1,0:T(8,128)(2,1)S(1)} %convolution_convert_fusion.4), channel_id=2, replica_groups=mesh['seq_0'=16,'seq_1'=4,'head'=8,'pair'=2] {'seq_1'}, dimensions={0}, use_global_device_ids=true | all-gather | bytes 163840 | tf_op jit(solution)/shard_map/all_gather | solution.py:25
  10.2 38.6 %all_gather.12 = bf16[16,1,128,128]{3,2,1,0:T(8,128)(2,1)S(1)} all-gather(bf16[1,1,128,128]{3,2,1,0:T(8,128)(2,1)S(1)} %fusion.104), channel_id=1, replica_groups=mesh['seq_0'=16,'seq_1'=4,'head'=8,'pair'=2] {'seq_0'}, dimensions={0}, use_global_device_ids=true | all-gather | bytes 557056 | tf_op jit(solution)/shard_map/all_gather | solution.py:25
  48.7 1.1 fusion.35
  49.9 1.1 multiply_reduce_fusion.1
  51.0 1.2 fusion.1
  52.2 17.6 %all-to-all-start = ((bf16[16,8,2048]{2,1,0:T(8,128)(2,1)}), bf16[16,8,2048]{2,1,0:T(8,128)(2,1)S(1)}, u32[]{:S(2)}, u32[]{:S(2)}) async-start(bf16[16,8,2048]{2,1,0:T(8,128)(2,1)} %fusion.1), calls=%async_computation | async-start | bytes 1048576 | tf_op jit(solution)/shard_map/all_to_all | solution.py:42
  70.0 0.1 reshape.269
  70.1 0.1 reduce_window_sum.12
  70.2 0.2 select_reduce_fusion
  70.4 0.1 reduce_sum.68
  70.5 0.1 convert_reduce_fusion.1
  70.6 16.4 %all-to-all-done = bf16[16,8,2048]{2,1,0:T(8,128)(2,1)S(1)} async-done(((bf16[16,8,2048]{2,1,0:T(8,128)(2,1)}), bf16[16,8,2048]{2,1,0:T(8,128)(2,1)S(1)}, u32[]{:S(2)}, u32[]{:S(2)}) %all-to-all-start) | async-done | bytes 524320 | tf_op jit(solution)/shard_map/all_to_all | solution.py:42
  87.1 0.1 multiply_reduce_fusion
  87.3 0.5 fusion
  87.8 1.6 copy.28
  89.4 0.5 broadcast.247
  89.9 7.8 %reduce.3 = bf16[256,2048]{1,0:T(8,128)(2,1)} reduce(bf16[256,1,2048]{2,1,0:T(2,128)(2,1)S(1)} %bitcast.91, bf16[]{:T(256)} %broadcast.247), dimensions={1}, to_apply=%bitcast.89.reduce_sub_computation | reduce | bytes 2097154
  97.7 1.9 reshape.306
  99.6 61.3 %all_to_all.32 = bf16[64,2,4096]{2,1,0:T(2,128)(2,1)} all-to-all(bf16[64,2,4096]{2,1,0:T(2,128)(2,1)S(1)} %reshape.306), channel_id=1, replica_groups=mesh['seq_0'=16,'seq_1'=4,'head'=8,'pair'=2] {'seq_0','seq_1'}, dimensions={0} | all-to-all | bytes 2097152 | tf_op jit(solution)/shard_map/all_to_all | solution.py:159
  160.8 6.5 %reshape.307 = bf16[256,1,2048]{2,1,0:T(2,128)(2,1)S(1)} reshape(bf16[64,2,4096]{2,1,0:T(2,128)(2,1)} %all_to_all.32) | data formatting | bytes 2097152
  167.3 0.6 copy.27
  167.9 0.3 broadcast_in_dim.38
  168.2 6.0 %all_to_all.33 = bf16[2,1,256,2048]{3,2,1,0:T(8,128)(2,1)} all-to-all(bf16[2,1,256,2048]{3,2,1,0:T(8,128)(2,1)S(1)} %broadcast_in_dim.38), channel_id=1, replica_groups=mesh['seq_0'=16,'seq_1'=4,'head'=8,'pair'=2] {'pair'}, dimensions={0} | all-to-all | bytes 4194304 | tf_op jit(solution)/shard_map/all_to_all | solution.py:54
  174.2 3.4 %reshape_reshape_reshape.3 = bf16[128,8192]{1,0:T(8,128)(2,1)S(1)} reshape(bf16[2,1,256,2048]{3,2,1,0:T(8,128)(2,1)} %all_to_all.33) | data formatting | bytes 4194304 | tf_op jit(solution)/shard_map/reshape;reshape;reshape | solution.py:167
  177.6 1.5 fusion.162
  179.1 1.4 reshape.270
  180.5 2.1 fusion.10
  182.6 3.2 %convolution_convert_fusion.1 = bf16[256,2048]{1,0:T(8,128)(2,1)S(1)} fusion(bf16[2,384,2048]{2,1,0:T(8,128)(2,1)} %param.23, bf16[256,2048]{1,0:T(8,128)(2,1)S(1)} %reshape.270, bf16[2,2048,384]{2,1,0:T(8,128)(2,1)} %param.22, f32[256,384]{1,0:T(8,128)S(1)} %fusion.10), kind=kOutput, calls=%fused_computation.2 | convolution fusion | flops 806420480 | bytes 5636096 | tf_op jit(solution)/shard_map/dot_general | solution.py:176
  185.8 1.2 reshape.271
  187.1 0.2 copy-done.1
  187.3 0.4 reshape.272
  187.7 2.1 fusion.5
  189.8 3.2 %convolution_convert_fusion = bf16[256,2048]{1,0:T(8,128)(2,1)S(1)} fusion(bf16[2,384,2048]{2,1,0:T(8,128)(2,1)} %param.23, bf16[256,2048]{1,0:T(8,128)(2,1)S(1)} %reshape.272, bf16[2,2048,384]{2,1,0:T(8,128)(2,1)} %param.22, f32[256,384]{1,0:T(8,128)S(1)} %fusion.5), kind=kOutput, calls=%fused_computation.1 | convolution fusion | flops 806420480 | bytes 5636096 | tf_op jit(solution)/shard_map/dot_general | solution.py:176
  193.0 1.2 reshape.273
  194.2 1.7 pad_maximum_fusion
  195.9 2.9 %convert_element_type.240 = bf16[2,256,2048]{2,1,0:T(8,128)(2,1)} reshape(bf16[128,8192]{1,0:T(8,128)(2,1)S(1)} %pad_maximum_fusion) | data formatting | bytes 4194304 | tf_op jit(solution)/shard_map/convert_element_type | solution.py:181
  198.8 6.6 %all_to_all.34 = bf16[2,256,2048]{2,1,0:T(8,128)(2,1)S(1)} all-to-all(bf16[2,256,2048]{2,1,0:T(8,128)(2,1)} %convert_element_type.240), channel_id=1, replica_groups=mesh['seq_0'=16,'seq_1'=4,'head'=8,'pair'=2] {'pair'}, dimensions={0} | all-to-all | bytes 4194304 | tf_op jit(solution)/shard_map/all_to_all | solution.py:42
  205.4 1.7 reduce_sum.71
  207.1 2.3 all_to_all.24
  209.4 5.4 %all-to-all-start.4 = ((bf16[64,4,2048]{2,1,0:T(4,128)(2,1)}), bf16[64,4,2048]{2,1,0:T(4,128)(2,1)S(1)}, u32[]{:S(2)}, u32[]{:S(2)}) async-start(bf16[64,4,2048]{2,1,0:T(4,128)(2,1)} %all_to_all.24), calls=%async_computation.4 | async-start | bytes 2097152 | tf_op jit(solution)/shard_map/all_to_all | solution.py:185
  214.8 0.1 mul.105
  214.9 0.1 copy.20
  215.0 53.7 %all-to-all-done.4 = bf16[64,4,2048]{2,1,0:T(4,128)(2,1)S(1)} async-done(((bf16[64,4,2048]{2,1,0:T(4,128)(2,1)}), bf16[64,4,2048]{2,1,0:T(4,128)(2,1)S(1)}, u32[]{:S(2)}, u32[]{:S(2)}) %all-to-all-start.4) | async-done | bytes 1048608 | tf_op jit(solution)/shard_map/all_to_all | solution.py:185
  268.8 0.3 all_to_all.26
  269.0 0.7 gather_fusion
  269.8 0.3 fusion.46
  270.1 0.6 fusion.71
  (25 shorter events, 0.5 us)
Async XLA Ops:
  0.0 51.0 %copy-start = (bf16[128,2048]{1,0:T(8,128)(2,1)S(1)}, bf16[128,2048]{1,0:T(8,128)(2,1)}, u32[]{:S(2)}) copy-start(bf16[128,2048]{1,0:T(8,128)(2,1)} %param.17) | copy-start | bytes 1572868
  0.0 51.0 %copy-start.6 = (f32[128]{0:T(128)S(1)}, f32[128]{0:T(128)}, u32[]{:S(2)}) copy-start(f32[128]{0:T(128)} %param.16) | copy-start | bytes 1540
  10.2 59.7 %copy-start.4 = (s32[16,8]{0,1:T(8,128)S(1)}, s32[16,8]{0,1:T(8,128)}, u32[]{:S(2)}) copy-start(s32[16,8]{0,1:T(8,128)} %param.19) | copy-start | bytes 1540
  49.8 37.3 %copy-start.2 = (bf16[8,2048]{1,0:T(8,128)(2,1)S(1)}, bf16[8,2048]{1,0:T(8,128)(2,1)}, u32[]{:S(2)}) copy-start(bf16[8,2048]{1,0:T(8,128)(2,1)} %param.15) | copy-start | bytes 98308
  49.9 37.4 %copy-start.3 = (f32[2048]{0:T(1024)S(1)}, f32[2048]{0:T(1024)}, u32[]{:S(2)}) copy-start(f32[2048]{0:T(1024)} %param.18) | copy-start | bytes 24580
  52.2 34.8 %all-to-all-start = ((bf16[16,8,2048]{2,1,0:T(8,128)(2,1)}), bf16[16,8,2048]{2,1,0:T(8,128)(2,1)S(1)}, u32[]{:S(2)}, u32[]{:S(2)}) async-start(bf16[16,8,2048]{2,1,0:T(8,128)(2,1)} %fusion.1), calls=%async_computation | async-start | bytes 1048576 | tf_op jit(solution)/shard_map/all_to_all | solution.py:42
  185.8 1.5 copy-start.1
  207.1 7.8 %copy-start.5 = (f32[16,8]{0,1:T(8,128)S(1)}, f32[16,8]{0,1:T(8,128)}, u32[]{:S(2)}) copy-start(f32[16,8]{0,1:T(8,128)} %param.20) | copy-start | bytes 1540
  209.4 59.4 %all-to-all-start.4 = ((bf16[64,4,2048]{2,1,0:T(4,128)(2,1)}), bf16[64,4,2048]{2,1,0:T(4,128)(2,1)S(1)}, u32[]{:S(2)}, u32[]{:S(2)}) async-start(bf16[64,4,2048]{2,1,0:T(4,128)(2,1)} %all_to_all.24), calls=%async_computation.4 | async-start | bytes 2097152 | tf_op jit(solution)/shard_map/all_to_all | solution.py:185
where the time goes:
time: 274 us; the launch traced here: 271 us
  blocking collectives  122 us (45%)
  waiting for transfers between devices  70.1 us (26%)
  local copies, waits for them, and re-layouts  27.4 us (10%)
  starting transfers between devices  23 us (8%)
  matrix products  15.8 us (6%)
  other arithmetic  12.6 us (5%)
    all_to_all x1, blocking collectives, body(): lax.all_to_all(own_buffer, SEQ, split_axis=1, concat_axis=1, tiled=True)  61.3 us
    all_to_all x1, waiting for transfers between devices, body(): lax.all_to_all(expert_out, SEQ, split_axis=0, concat_axis=0, tiled=True)  53.7 us
    all_gather x2, blocking collectives, entering(): pieces = lax.all_gather(total.astype(jnp.bfloat16), axis)  47.7 us
    all_to_all x1, starting transfers between devices, sent_and_summed(): blocks = lax.all_to_all(split_up(shard, dim, size), axis, 0, 0, tiled=True)  17.6 us
    all_to_all x1, waiting for transfers between devices, sent_and_summed(): blocks = lax.all_to_all(split_up(shard, dim, size), axis, 0, 0, tiled=True)  16.4 us
    unnamed x19, local copies, waits for them, and re-layouts  9.8 us
    unnamed x1, other arithmetic  7.78 us
    all_to_all x1, blocking collectives, sent_and_summed(): blocks = lax.all_to_all(split_up(shard, dim, size), axis, 0, 0, tiled=True)  6.62 us
  transfers between devices with their start and end apart: 2, of which 2 were waited for; matrix products, arithmetic and copies ran while one was open for 0% of the time, Pallas kernels for 0%

commit v1 on v0

v1 whole, which is shorter than its diff:
```python
import jax
import jax.numpy as jnp
from jax import lax
from jax.sharding import Mesh
from jax.sharding import PartitionSpec as P

HEAD_DIM = 128
LANES = 128
ROUTE_BLOCK = 8
SEQ = ("seq_0", "seq_1")
SEQ_HEAD_PAIR = ("seq_0", "seq_1", "head", "pair")
SEQ_HEAD = ("seq_0", "seq_1", "head")
EPSILON = 1e-06


def rms_scale(values, gain_vec):
    mean_sq = jnp.mean(values * values, axis=-1, keepdims=True)
    return values * lax.rsqrt(mean_sq + EPSILON) * gain_vec


def entering_state(local_state):
    size = lax.axis_size(SEQ)
    rows, width = local_state.shape
    pieces = local_state.astype(jnp.bfloat16).reshape(size, rows // size, width)
    gathered = lax.all_to_all(pieces, SEQ, 0, 0, tiled=True)
    place = jnp.arange(size)
    earlier = (place[:, None] > place[None, :]).astype(jnp.bfloat16)
    sums = jnp.dot(
        earlier, gathered.reshape(size, -1), preferred_element_type=jnp.float32
    )
    back = lax.all_to_all(
        sums.astype(jnp.bfloat16).reshape(pieces.shape), SEQ, 0, 0, tiled=True
    )
    return back.reshape(rows, width)


def with_routing(rows, expert_ids, weights):
    count, top = expert_ids.shape
    high = weights.astype(jnp.bfloat16)
    low = (weights - high.astype(jnp.float32)).astype(jnp.bfloat16)
    tail = jnp.concatenate(
        [
            expert_ids.astype(jnp.bfloat16),
            high,
            low,
            jnp.zeros((count, LANES - 3 * top), jnp.bfloat16),
        ],
        axis=1,
    )
    return jnp.concatenate([rows, tail], axis=1)


def body(
    query_rows,
    all_head_keys,
    value_rows,
    stream,
    attn_gain,
    out_weight,
    moe_gain,
    routes,
    gate_weights,
    w_gate,
    w_up,
    w_down,
):
    length = query_rows.shape[0]
    local_state = jnp.einsum(
        "tz,td->zd", all_head_keys, value_rows, preferred_element_type=jnp.float32
    )
    previous = entering_state(local_state)
    causal = jnp.arange(length)[:, None] >= jnp.arange(length)[None, :]
    scores = jnp.where(
        causal,
        jnp.einsum("tk,sk->ts", query_rows, all_head_keys, preferred_element_type=jnp.float32),
        0.0,
    )
    mixed = jnp.dot(scores, value_rows.astype(jnp.float32))
    mixed = mixed + jnp.dot(query_rows, previous, preferred_element_type=jnp.float32)
    attn_normed = rms_scale(mixed, attn_gain[None, :]).astype(jnp.bfloat16)
    partial_rows = jnp.dot(attn_normed, out_weight, preferred_element_type=jnp.float32)
    projected = lax.psum_scatter(
        partial_rows.astype(jnp.bfloat16), ("head", "pair"), scatter_dimension=0, tiled=True
    )
    block_rows, model_width = stream.shape
    residual = stream.astype(jnp.float32) + projected.astype(jnp.float32)
    moe_input = rms_scale(residual, moe_gain).astype(jnp.bfloat16)

    core = lax.axis_index("pair")
    my_routes = lax.dynamic_slice_in_dim(routes, core * block_rows, block_rows, 0)
    my_weights = lax.dynamic_slice_in_dim(gate_weights, core * block_rows, block_rows, 0)
    packed = with_routing(moe_input, my_routes, my_weights)
    plane = lax.all_gather(packed, SEQ, tiled=True)
    plane = lax.all_gather(plane, "pair", tiled=True)
    tokens = plane[:, :model_width]
    routing = plane[:, model_width:].astype(jnp.float32)
    top = routes.shape[1]
    ids = routing[:, :top]
    weights = routing[:, top : 2 * top] + routing[:, 2 * top : 3 * top]

    experts_here = w_gate.shape[0]
    first = lax.axis_index(SEQ) * experts_here
    hidden = []
    for expert in range(experts_here):
        named = ids == (first + expert).astype(jnp.float32)
        weight = jnp.sum(jnp.where(named, weights, 0.0), axis=1, keepdims=True)
        gate_part = jnp.dot(tokens, w_gate[expert], preferred_element_type=jnp.float32)
        up_part = jnp.dot(tokens, w_up[expert], preferred_element_type=jnp.float32)
        hidden.append((jax.nn.silu(gate_part) * up_part * weight).astype(jnp.bfloat16))
    outputs = jnp.dot(
        jnp.concatenate(hidden, axis=1),
        w_down.reshape(-1, model_width),
        preferred_element_type=jnp.float32,
    ).astype(jnp.bfloat16)
    outputs = lax.psum_scatter(outputs, "pair", scatter_dimension=0, tiled=True)
    combined = lax.psum_scatter(outputs, SEQ, scatter_dimension=0, tiled=True)
    return (residual + combined.astype(jnp.float32)).astype(jnp.bfloat16)


def solution(mesh):
    split = Mesh(
        mesh.devices.reshape(16, 4, mesh.shape["head"], mesh.shape["pair"]),
        ("seq_0", "seq_1", "head", "pair"),
    )
    placed = (
        P(SEQ, ("head", "pair")),
        P(SEQ, ("head", "pair")),
        P(SEQ, ("head", "pair")),
        P(SEQ_HEAD_PAIR, None),
        P(("head", "pair")),
        P(("head", "pair"), None),
        P(),
        P(SEQ_HEAD, None),
        P(SEQ_HEAD, None),
        P(SEQ, None, "pair"),
        P(SEQ, None, "pair"),
        P(SEQ, "pair", None),
    )
    return jax.shard_map(
        body, mesh=split, in_specs=placed, out_specs=P(SEQ_HEAD_PAIR, None), check_vma=False
    )
```

time: 274 us -> 1070 us (3.91); the launches traced: 271 us -> 1050 us
  waiting for transfers between devices: 70.1 us -> 972 us
  blocking collectives: 122 us -> 33.4 us
  local copies, waits for them, and re-layouts: 27.4 us -> 1.67 us
  starting transfers between devices: 23 us -> 6.5 us
  between operations: 0.24 us -> 13.3 us
    reduce_scatter x0 -> x3, waiting for transfers between devices: none -> 784 us  [the longest x1 701 us: body(): combined = lax.psum_scatter(outputs, SEQ, scatter_dimension=0, tiled=True)]
    all_gather x0 -> x2, waiting for transfers between devices: none -> 177 us  [the longest x1 141 us: body(): plane = lax.all_gather(packed, SEQ, tiled=True)]
    all_to_all x2 -> x1, waiting for transfers between devices: 70.1 us -> 10.6 us  [entering_state(): lax.all_to_all(sums.astype(jnp.bfloat16).reshape(pieces.shape), SEQ, 0, 0...]
    all_gather x2 -> x0, blocking collectives: 47.7 us -> none  [entering(): pieces = lax.all_gather(total.astype(jnp.bfloat16), axis)]
    all_to_all x3 -> x1, blocking collectives: 73.9 us -> 33.4 us  [entering_state(): gathered = lax.all_to_all(pieces, SEQ, 0, 0, tiled=True)]
    all_to_all x2 -> x1, starting transfers between devices: 23 us -> 6.12 us  [entering_state(): lax.all_to_all(sums.astype(jnp.bfloat16).reshape(pieces.shape), SEQ, 0, 0...]
  transfers between devices with their start and end apart: 2 -> 6, of which waited for: 2 -> 6; matrix products, arithmetic and copies ran while one was open for 0% -> 0% of each run, Pallas kernels for 0% -> 0%
where the time goes in v1:
time: 1070 us; the launch traced here: 1050 us
  waiting for transfers between devices  972 us (91%)
  blocking collectives  33.4 us (3%)
  matrix products  21.4 us (2%)
  between operations  13.3 us (1%)
    reduce_scatter x1, waiting for transfers between devices, body(): combined = lax.psum_scatter(outputs, SEQ, scatter_dimension=0, tiled=True)  701 us
    all_gather x1, waiting for transfers between devices, body(): plane = lax.all_gather(packed, SEQ, tiled=True)  141 us
    reduce_scatter x1, waiting for transfers between devices, body(): lax.psum_scatter(partial_rows.astype(jnp.bfloat16), ('head', 'pair'), sca...  56 us
    all_gather x1, waiting for transfers between devices, body(): plane = lax.all_gather(plane, 'pair', tiled=True)  36.3 us
    all_to_all x1, blocking collectives, entering_state(): gathered = lax.all_to_all(pieces, SEQ, 0, 0, tiled=True)  33.4 us
    reduce_scatter x1, waiting for transfers between devices, body(): outputs = lax.psum_scatter(outputs, 'pair', scatter_dimension=0, tiled=True)  27.1 us
  transfers between devices with their start and end apart: 6, of which 6 were waited for; matrix products, arithmetic and copies ran while one was open for 0% of the time, Pallas kernels for 0%

profile of v1, /device:TPU:7, one launch (start us, length us, event | category | flops | bytes accessed | tf_op | source)
XLA Modules:
  0.0 1052.9 jit_solution(5646279656908020690)
XLA Ops:
  6.5 0.0 copy-start
  6.5 1.1 convolution_convert_fusion.3
  7.7 33.4 %all_to_all.10 = bf16[64,2,128]{2,1,0:T(2,128)(2,1)S(1)} all-to-all(bf16[64,2,128]{2,1,0:T(2,128)(2,1)S(1)} %bitcast.37), channel_id=1, replica_groups=mesh['seq_0'=16,'seq_1'=4,'head'=8,'pair'=2] {'seq_0','seq_1'}, dimensions={0} | all-to-all | bytes 65536 | tf_op jit(solution)/shard_map/all_to_all | solution.py:25
  41.0 0.1 convolution_convert_fusion.2
  41.1 0.6 reshape.37
  41.8 6.1 all-to-all-start.1
  47.9 0.0 reduce-scatter.4.cloned.1.call-start
  48.0 1.1 fusion.28
  49.1 10.6 %all-to-all-done.1 = bf16[64,2,128]{2,1,0:T(2,128)(2,1)S(1)} async-done(((bf16[64,2,128]{2,1,0:T(2,128)(2,1)}), bf16[64,2,128]{2,1,0:T(2,128)(2,1)S(1)}, u32[]{:S(2)}, u32[]{:S(2)}) %all-to-all-start.1) | async-done | bytes 32800 | tf_op jit(solution)/shard_map/all_to_all | solution.py:31
  59.7 1.0 multiply_reduce_fusion.1
  60.6 2.2 convolution_convert_fusion.1
  62.9 0.0 reduce-scatter.4.cloned.1.call-update
  62.9 0.0 all-gather.3.cloned.1.call-start
  63.0 0.0 copy-done.4
  63.0 0.1 constant_dynamic-slice_fusion.1
  63.1 0.1 copy.15
  63.1 0.0 copy-done.5
  63.1 0.1 constant_dynamic-slice_fusion
  63.2 0.1 copy.16
  63.3 56.0 %reduce-scatter.4.cloned.1.call-done = bf16[8,2048]{1,0:T(8,128)(2,1)} async-done(((bf16[128,2048]{1,0:T(8,128)(2,1)}), bf16[8,2048]{1,0:T(8,128)(2,1)}) %reduce-scatter.4.cloned.1.call-update) | async-done | bytes 32784 | tf_op jit(solution)/shard_map/reduce_scatter | solution.py:82
  119.2 0.0 copy-done.1
  119.3 0.9 multiply_reduce_fusion
  120.2 0.8 multiply_convert_fusion.2
  121.0 0.7 concatenate.6
  121.7 0.0 all-gather.3.cloned.1.call-update
  121.7 0.0 all-gather.5.cloned.1.call-start
  121.8 140.7 %all-gather.3.cloned.1.call-done = bf16[512,2176]{1,0:T(8,128)(2,1)} async-done(((bf16[8,2176]{1,0:T(8,128)(2,1)}), bf16[512,2176]{1,0:T(8,128)(2,1)}) %all-gather.3.cloned.1.call-update) | async-done | bytes 2228240 | tf_op jit(solution)/shard_map/all_gather | solution.py:93
  262.5 0.0 all-gather.5.cloned.1.call-update
  262.5 0.2 reduce-scatter.6.cloned.1.call-start
  262.8 36.3 %all-gather.5.cloned.1.call-done = bf16[1024,2176]{1,0:T(8,128)(2,1)} async-done(((bf16[512,2176]{1,0:T(8,128)(2,1)}), bf16[1024,2176]{1,0:T(8,128)(2,1)}) %all-gather.5.cloned.1.call-update) | async-done | bytes 4456464 | tf_op jit(solution)/shard_map/all_gather | solution.py:94
  299.1 1.0 slice_convert_fusion
  300.1 0.0 slice-start
  300.1 0.6 select_reduce_fusion.1
  300.7 0.0 slice-start.1
  300.7 0.0 copy-start.6
  300.7 4.8 fusion.2
  305.6 0.0 copy-start.7
  305.6 1.9 fusion.6
  307.5 0.0 copy-done.7
  307.5 2.1 multiply_convert_fusion
  309.5 2.1 multiply_convert_fusion.1
  311.6 5.1 convolution_convert_fusion
  316.7 0.0 reduce-scatter.6.cloned.1.call-update
  316.7 0.0 reduce-scatter.8.cloned.1.call-start
  316.8 27.1 %reduce-scatter.6.cloned.1.call-done = bf16[512,2048]{1,0:T(8,128)(2,1)} async-done(((bf16[1024,2048]{1,0:T(8,128)(2,1)}), bf16[512,2048]{1,0:T(8,128)(2,1)}) %reduce-scatter.6.cloned.1.call-update) | async-done | bytes 2097168 | tf_op jit(solution)/shard_map/reduce_scatter | solution.py:115
  343.9 0.0 reduce-scatter.8.cloned.1.call-update
  343.9 701.1 %reduce-scatter.8.cloned.1.call-done = bf16[8,2048]{1,0:T(8,128)(2,1)} async-done(((bf16[512,2048]{1,0:T(8,128)(2,1)}), bf16[8,2048]{1,0:T(8,128)(2,1)}) %reduce-scatter.8.cloned.1.call-update) | async-done | bytes 32784 | tf_op jit(solution)/shard_map/reduce_scatter | solution.py:116
  1045.0 1.4 add_convert_fusion
  (17 shorter events, 0.1 us)
Async XLA Ops:
  6.5 305.1 %copy-start = (bf16[2,384,2048]{2,1,0:T(8,128)(2,1)S(1)}, bf16[2,384,2048]{2,1,0:T(8,128)(2,1)}, u32[]{:S(2)}) copy-start(bf16[2,384,2048]{2,1,0:T(8,128)(2,1)} %param.23) | copy-start | bytes 9437188
  6.5 56.4 %copy-start.4 = (s32[16,8]{0,1:T(8,128)S(1)}, s32[16,8]{0,1:T(8,128)}, u32[]{:S(2)}) copy-start(s32[16,8]{0,1:T(8,128)} %param.19) | copy-start | bytes 1540
  6.5 56.6 %copy-start.5 = (f32[16,8]{0,1:T(8,128)S(1)}, f32[16,8]{0,1:T(8,128)}, u32[]{:S(2)}) copy-start(f32[16,8]{0,1:T(8,128)} %param.20) | copy-start | bytes 1540
  6.5 112.7 %copy-start.1 = (bf16[8,2048]{1,0:T(8,128)(2,1)S(1)}, bf16[8,2048]{1,0:T(8,128)(2,1)}, u32[]{:S(2)}) copy-start(bf16[8,2048]{1,0:T(8,128)(2,1)} %param.15) | copy-start | bytes 98308
  6.5 113.6 %copy-start.3 = (f32[2048]{0:T(1024)S(1)}, f32[2048]{0:T(1024)}, u32[]{:S(2)}) copy-start(f32[2048]{0:T(1024)} %param.18) | copy-start | bytes 24580
  41.8 17.9 %all-to-all-start.1 = ((bf16[64,2,128]{2,1,0:T(2,128)(2,1)}), bf16[64,2,128]{2,1,0:T(2,128)(2,1)S(1)}, u32[]{:S(2)}, u32[]{:S(2)}) async-start(bf16[64,2,128]{2,1,0:T(2,128)(2,1)} %reshape.37), calls=%async_computation.1 | async-start | bytes 65536 | tf_op jit(solution)/shard_map/all_to_all | solution.py:31
  47.9 71.3 %reduce-scatter.4.cloned.1.call-start = ((), (), s32[]{:S(2)}) async-start(), calls=%async_computation.5 | async-start | bytes 557056 | tf_op jit(solution)/shard_map/reduce_scatter | solution.py:82
  62.9 199.6 %all-gather.3.cloned.1.call-start = ((), (), s32[]{:S(2)}) async-start(), calls=%async_computation.6 | async-start | bytes 2263040 | tf_op jit(solution)/shard_map/all_gather | solution.py:93
  121.7 177.4 %all-gather.5.cloned.1.call-start = ((), (), s32[]{:S(2)}) async-start(), calls=%async_computation.7 | async-start | bytes 6684672 | tf_op jit(solution)/shard_map/all_gather | solution.py:94
  262.5 81.3 %reduce-scatter.6.cloned.1.call-start = ((), (), s32[]{:S(2)}) async-start(), calls=%async_computation.8 | async-start | bytes 6291456 | tf_op jit(solution)/shard_map/reduce_scatter | solution.py:115
  300.1 5.5 slice-start
  300.7 4.9 slice-start.1
  300.7 4.9 copy-start.6
  305.6 1.9 copy-start.7
  316.7 728.3 %copy-start.2 = (bf16[8,2048]{1,0:T(8,128)(2,1)S(1)}, bf16[8,2048]{1,0:T(8,128)(2,1)}, u32[]{:S(2)}) copy-start(bf16[8,2048]{1,0:T(8,128)(2,1)} %reduce-scatter.4.cloned.1.call-done) | copy-start | bytes 98308
  316.7 728.2 %reduce-scatter.8.cloned.1.call-start = ((), (), s32[]{:S(2)}) async-start(), calls=%async_computation.9 | async-start | bytes 2129920 | tf_op jit(solution)/shard_map/reduce_scatter | solution.py:116
Sparse Core Ops, SparseCore 0:
  63.0 56.1 reduce-scatter.3
  123.4 139.0 all-gather.2
  265.2 33.8 all-gather.4
  316.8 26.9 reduce-scatter.5
  349.3 695.6 reduce-scatter.7

commit v2 on v1

v2 whole, which is shorter than its diff:
```python
import jax
import jax.numpy as jnp
from jax import lax
from jax.sharding import Mesh
from jax.sharding import PartitionSpec as P

LANES = 128
CAP = 2
Z = ("zh", "zl")
NEAR = ("zl", "x")
SEQ = ("zh", "zl", "x")
SEQ_HEAD_PAIR = ("zh", "zl", "x", "head", "pair")
SEQ_HEAD = ("zh", "zl", "x", "head")
SWAP = ((0, 1), (1, 0))
EPSILON = 1e-06


def rms_scale(values, gain_vec):
    mean_sq = jnp.mean(values * values, axis=-1, keepdims=True)
    return values * lax.rsqrt(mean_sq + EPSILON) * gain_vec


def to_each(shard, axis):
    copies = jnp.broadcast_to(shard[None], (lax.axis_size(axis), *shard.shape))
    return lax.all_to_all(copies, axis, 0, 0, tiled=True)


def entering_state(local_state):
    rows, width = local_state.shape
    across = lax.axis_size("x")
    along = lax.axis_size(Z)
    parts = local_state.astype(jnp.bfloat16).reshape(across, rows // across, width)
    parts = lax.all_to_all(parts, "x", 0, 0, tiled=True).astype(jnp.float32)
    totals = to_each(jnp.sum(parts, axis=0).astype(jnp.bfloat16), Z).astype(jnp.float32)
    passed = (jnp.arange(along) < lax.axis_index(Z))[:, None, None]
    running = jnp.sum(jnp.where(passed, totals, 0.0), axis=0)
    entering = []
    for place in range(across):
        entering.append(running.astype(jnp.bfloat16))
        running = running + parts[place]
    back = lax.all_to_all(jnp.stack(entering), "x", 0, 0, tiled=True)
    return back.reshape(rows, width)


def two_terms(values):
    high = lax.reduce_precision(values, exponent_bits=8, mantissa_bits=7)
    return high.astype(jnp.bfloat16), (values - high).astype(jnp.bfloat16)


def with_routing(rows, expert_ids, weights):
    count, top = expert_ids.shape
    high, low = two_terms(weights)
    tail = jnp.concatenate(
        [
            expert_ids.astype(jnp.bfloat16),
            high,
            low,
            jnp.zeros((count, LANES - 3 * top), jnp.bfloat16),
        ],
        axis=1,
    )
    return jnp.concatenate([rows, tail], axis=1)


def slot_matrices(ids, weights, first, experts, block_rows):
    count = ids.shape[0]
    blocks = count // block_rows
    wanted = first + jnp.arange(experts, dtype=jnp.int32)
    named = wanted.astype(jnp.float32)[:, None, None] == ids.T[None]
    chosen = jnp.sum(named.astype(jnp.float32), axis=1)
    weight = jnp.sum(jnp.where(named, weights.T[None], 0.0), axis=1)
    row = jnp.arange(count)
    same_block = row[:, None] // block_rows == row[None, :] // block_rows
    ahead = (same_block & (row[:, None] < row[None, :])).astype(jnp.bfloat16)
    rank = jnp.dot(chosen.astype(jnp.bfloat16), ahead, preferred_element_type=jnp.float32)
    code = jnp.where(chosen > 0.0, rank, -1.0)
    per_expert = blocks * CAP
    slot = jnp.arange(per_expert)
    in_block = slot[:, None] // CAP == row[None, :] // block_rows
    slot_rank = (slot % CAP).astype(jnp.float32)
    fills = in_block[None] & (code[:, None, :] == slot_rank[None, :, None])
    fills = fills.reshape(experts * per_expert, count)
    added = jnp.broadcast_to(weight[:, None, :], (experts, per_expert, count))
    added = jnp.where(fills, added.reshape(fills.shape), 0.0)
    return fills.astype(jnp.bfloat16), added


def body(
    query_rows,
    all_head_keys,
    value_rows,
    stream,
    attn_gain,
    out_weight,
    moe_gain,
    routes,
    gate_weights,
    w_gate,
    w_up,
    w_down,
):
    length, head_width = query_rows.shape
    block_rows, model_width = stream.shape
    heads = lax.axis_size("head")
    core = lax.axis_index("pair")
    other_weight = lax.ppermute(out_weight, "pair", SWAP)

    local_state = jnp.einsum(
        "tz,td->zd", all_head_keys, value_rows, preferred_element_type=jnp.float32
    )
    previous = entering_state(local_state)
    causal = jnp.arange(length)[:, None] >= jnp.arange(length)[None, :]
    scores = jnp.where(
        causal,
        jnp.einsum("tk,sk->ts", query_rows, all_head_keys, preferred_element_type=jnp.float32),
        0.0,
    )
    mixed = jnp.dot(scores, value_rows.astype(jnp.float32))
    mixed = mixed + jnp.dot(query_rows, previous, preferred_element_type=jnp.float32)
    attn_normed = rms_scale(mixed, attn_gain[None, :]).astype(jnp.bfloat16)

    by_core = attn_normed.reshape(heads, 2, block_rows, head_width)
    kept = jnp.where(core == 0, by_core[:, 0], by_core[:, 1]).reshape(-1, head_width)
    given = jnp.where(core == 0, by_core[:, 1], by_core[:, 0]).reshape(-1, head_width)
    taken = lax.ppermute(given, "pair", SWAP)
    partial_rows = jnp.dot(kept, out_weight, preferred_element_type=jnp.float32) + jnp.dot(
        taken, other_weight, preferred_element_type=jnp.float32
    )
    partial_rows = partial_rows.astype(jnp.bfloat16).reshape(heads, block_rows, model_width)
    partial_rows = lax.all_to_all(partial_rows, "head", 0, 0, tiled=True)
    projected = jnp.sum(partial_rows.astype(jnp.float32), axis=0)
    residual = stream.astype(jnp.float32) + projected
    moe_input = rms_scale(residual, moe_gain).astype(jnp.bfloat16)

    top = routes.shape[1]
    my_routes = lax.dynamic_slice_in_dim(routes, core * block_rows, block_rows, 0)
    my_weights = lax.dynamic_slice_in_dim(gate_weights, core * block_rows, block_rows, 0)
    packed = to_each(with_routing(moe_input, my_routes, my_weights), "zh")
    blocks = packed.shape[0]
    packed = packed.reshape(blocks * block_rows, -1)
    routing = packed[:, model_width : model_width + 3 * top].astype(jnp.float32)
    weights = routing[:, top : 2 * top] + routing[:, 2 * top :]
    experts_here = w_gate.shape[0]
    near = lax.axis_size(NEAR)
    fills, added = slot_matrices(
        routing[:, :top],
        weights,
        lax.axis_index("zh") * near * experts_here,
        near * experts_here,
        block_rows,
    )
    slots = jnp.dot(fills, packed[:, :model_width], preferred_element_type=jnp.float32)
    slots = slots.astype(jnp.bfloat16).reshape(near, -1, model_width)
    own = lax.all_to_all(slots, NEAR, 0, 0, tiled=True)
    other = lax.ppermute(own, "pair", SWAP)

    per_expert = blocks * CAP
    for_own, for_other = [], []
    for expert in range(experts_here):
        span = slice(expert * per_expert, (expert + 1) * per_expert)
        rows = jnp.concatenate(
            [own[:, span].reshape(-1, model_width), other[:, span].reshape(-1, model_width)]
        )
        gate_part = jnp.dot(rows, w_gate[expert], preferred_element_type=jnp.float32)
        up_part = jnp.dot(rows, w_up[expert], preferred_element_type=jnp.float32)
        activated = (jax.nn.silu(gate_part) * up_part).astype(jnp.bfloat16)
        result = jnp.dot(activated, w_down[expert], preferred_element_type=jnp.float32)
        half = near * per_expert
        for_own.append(result[:half].reshape(near, per_expert, model_width))
        for_other.append(
            result[half:].astype(jnp.bfloat16).reshape(near, per_expert, model_width)
        )
    from_other = lax.ppermute(jnp.concatenate(for_other, axis=1), "pair", SWAP)
    expert_out = jnp.concatenate(for_own, axis=1) + from_other.astype(jnp.float32)
    returned = lax.all_to_all(expert_out.astype(jnp.bfloat16), NEAR, 0, 0, tiled=True)
    returned = returned.reshape(-1, model_width)

    high, low = two_terms(added)
    sums = jnp.einsum("sr,sd->rd", high, returned, preferred_element_type=jnp.float32)
    sums = sums + jnp.einsum("sr,sd->rd", low, returned, preferred_element_type=jnp.float32)
    sums = sums.astype(jnp.bfloat16).reshape(blocks, block_rows, model_width)
    sums = lax.all_to_all(sums, "zh", 0, 0, tiled=True)
    combined = jnp.sum(sums.astype(jnp.float32), axis=0)
    return (residual + combined).astype(jnp.bfloat16)


def solution(mesh):
    split = Mesh(
        mesh.devices.reshape(8, 2, 4, mesh.shape["head"], mesh.shape["pair"]),
        SEQ_HEAD_PAIR,
    )
    placed = (
        P(SEQ, ("head", "pair")),
        P(SEQ, ("head", "pair")),
        P(SEQ, ("head", "pair")),
        P(SEQ_HEAD_PAIR, None),
        P(("head", "pair")),
        P(("head", "pair"), None),
        P(),
        P(SEQ_HEAD, None),
        P(SEQ_HEAD, None),
        P(SEQ, None, "pair"),
        P(SEQ, None, "pair"),
        P(SEQ, "pair", None),
    )
    return jax.shard_map(
        body, mesh=split, in_specs=placed, out_specs=P(SEQ_HEAD_PAIR, None), check_vma=False
    )
```

time: 1070 us -> 196 us (0.18)
  the two profiles are of different devices: /device:TPU:7 before, /device:TPU:2 now
where the time goes in v2:
time: 196 us; the launch traced here: 195 us
  waiting for transfers between devices  65.7 us (34%)
  blocking collectives  63.6 us (32%)
  starting transfers between devices  37 us (19%)
  matrix products  19.2 us (10%)
  local copies, waits for them, and re-layouts  5.17 us (3%)
  other arithmetic  4.32 us (2%)
    all_to_all x2, waiting for transfers between devices, to_each(): return lax.all_to_all(copies, axis, 0, 0, tiled=True)  31.4 us
    all_to_all x1, blocking collectives, body(): sums = lax.all_to_all(sums, 'zh', 0, 0, tiled=True)  26.8 us
    all_to_all x1, blocking collectives, entering_state(): parts = lax.all_to_all(parts, 'x', 0, 0, tiled=True).astype(jnp.float32)  19.5 us
    all_to_all x1, blocking collectives, body(): own = lax.all_to_all(slots, NEAR, 0, 0, tiled=True)  17.3 us
    all_to_all x1, waiting for transfers between devices, body(): lax.all_to_all(expert_out.astype(jnp.bfloat16), NEAR, 0, 0, tiled=True)  14.1 us
    all_to_all x1, waiting for transfers between devices, body(): partial_rows = lax.all_to_all(partial_rows, 'head', 0, 0, tiled=True)  12.2 us
    all_to_all x2, starting transfers between devices, to_each(): return lax.all_to_all(copies, axis, 0, 0, tiled=True)  11.7 us
    dot_general x2, matrix products, body(): jnp.dot(activated, w_down[expert], preferred_element_type=jnp.float32)  8.31 us
  transfers between devices with their start and end apart: 9, of which 7 were waited for; matrix products, arithmetic and copies ran while one was open for 2% of the time, Pallas kernels for 0%

profile of v2, /device:TPU:2, one launch (start us, length us, event | category | flops | bytes accessed | tf_op | source)
XLA Modules:
  0.0 195.2 jit_solution(16989543970945194393)
XLA Ops:
  0.0 1.0 convolution_convert_fusion.1
  1.0 19.5 %all_to_all.40 = bf16[4,32,128]{2,1,0:T(8,128)(2,1)S(1)} all-to-all(bf16[4,32,128]{2,1,0:T(8,128)(2,1)S(1)} %bitcast.116), channel_id=1, replica_groups=mesh['zh'=8,'zl'=2,'x'=4,'head'=8,'pair'=2] {'x'}, dimensions={0} | all-to-all | bytes 65536 | tf_op jit(solution)/shard_map/all_to_all | solution.py:33
  20.5 0.7 broadcast_in_dim.45
  21.2 8.1 %all-to-all-start.1 = ((bf16[16,32,128]{2,1,0:T(8,128)(2,1)}), bf16[16,32,128]{2,1,0:T(8,128)(2,1)S(1)}, u32[]{:S(2)}, u32[]{:S(2)}) async-start(bf16[16,32,128]{2,1,0:T(8,128)(2,1)} %broadcast_in_dim.45), calls=%async_computation.1 | async-start | bytes 262144 | tf_op jit(solution)/shard_map/all_to_all | solution.py:25
  29.3 1.9 collective-permute-start.1
  31.2 11.4 %all-to-all-done.1 = bf16[16,32,128]{2,1,0:T(8,128)(2,1)S(1)} async-done(((bf16[16,32,128]{2,1,0:T(8,128)(2,1)}), bf16[16,32,128]{2,1,0:T(8,128)(2,1)S(1)}, u32[]{:S(2)}, u32[]{:S(2)}) %all-to-all-start.1) | async-done | bytes 131104 | tf_op jit(solution)/shard_map/all_to_all | solution.py:25
  42.8 0.6 pad_maximum_fusion.9
  43.4 4.7 %all-to-all-start.2 = ((bf16[4,32,128]{2,1,0:T(8,128)(2,1)}), bf16[4,32,128]{2,1,0:T(8,128)(2,1)S(1)}, u32[]{:S(2)}, u32[]{:S(2)}) async-start(bf16[4,32,128]{2,1,0:T(8,128)(2,1)} %pad_maximum_fusion.9), calls=%async_computation.2 | async-start | bytes 65536 | tf_op jit(solution)/shard_map/all_to_all | solution.py:41
  48.1 1.0 fusion.40
  49.2 2.9 %all-to-all-done.2 = bf16[4,32,128]{2,1,0:T(8,128)(2,1)S(1)} async-done(((bf16[4,32,128]{2,1,0:T(8,128)(2,1)}), bf16[4,32,128]{2,1,0:T(8,128)(2,1)S(1)}, u32[]{:S(2)}, u32[]{:S(2)}) %all-to-all-start.2) | async-done | bytes 32800 | tf_op jit(solution)/shard_map/all_to_all | solution.py:41
  52.1 0.2 multiply_reduce_fusion.1
  52.4 0.7 multiply_convert_fusion.1
  53.1 1.9 collective-permute-start
  55.1 1.3 fusion.64
  56.4 0.9 fusion.3
  57.3 7.1 %all-to-all-start.3 = ((bf16[8,8,2048]{2,1,0:T(8,128)(2,1)}), bf16[8,8,2048]{2,1,0:T(8,128)(2,1)S(1)}, u32[]{:S(2)}, u32[]{:S(2)}) async-start(bf16[8,8,2048]{2,1,0:T(8,128)(2,1)} %fusion.3), calls=%async_computation.3 | async-start | bytes 524288 | tf_op jit(solution)/shard_map/all_to_all | solution.py:130
  64.7 12.2 %all-to-all-done.3 = bf16[8,8,2048]{2,1,0:T(8,128)(2,1)S(1)} async-done(((bf16[8,8,2048]{2,1,0:T(8,128)(2,1)}), bf16[8,8,2048]{2,1,0:T(8,128)(2,1)S(1)}, u32[]{:S(2)}, u32[]{:S(2)}) %all-to-all-start.3) | async-done | bytes 262176 | tf_op jit(solution)/shard_map/all_to_all | solution.py:130
  77.0 0.1 multiply_reduce_fusion
  77.2 0.1 concatenate.15
  77.3 0.7 broadcast_in_dim.48
  78.0 3.6 %all-to-all-start.4 = ((bf16[8,8,2176]{2,1,0:T(8,128)(2,1)}), bf16[8,8,2176]{2,1,0:T(8,128)(2,1)S(1)}, u32[]{:S(2)}, u32[]{:S(2)}) async-start(bf16[8,8,2176]{2,1,0:T(8,128)(2,1)} %broadcast_in_dim.48), calls=%async_computation.4 | async-start | bytes 557056 | tf_op jit(solution)/shard_map/all_to_all | solution.py:25
  81.9 19.9 %all-to-all-done.4 = bf16[8,8,2176]{2,1,0:T(8,128)(2,1)S(1)} async-done(((bf16[8,8,2176]{2,1,0:T(8,128)(2,1)}), bf16[8,8,2176]{2,1,0:T(8,128)(2,1)S(1)}, u32[]{:S(2)}, u32[]{:S(2)}) %all-to-all-start.4) | async-done | bytes 278560 | tf_op jit(solution)/shard_map/all_to_all | solution.py:25
  102.0 0.1 fusion.56
  102.2 0.2 convolution_select_fusion.1
  102.4 0.1 fusion.55
  102.5 0.4 convolution_convert_fusion
  102.9 17.3 %all_to_all.41 = bf16[8,32,2048]{2,1,0:T(8,128)(2,1)S(1)} all-to-all(bf16[8,32,2048]{2,1,0:T(8,128)(2,1)S(1)} %bitcast.97), channel_id=1, replica_groups=mesh['zh'=8,'zl'=2,'x'=4,'head'=8,'pair'=2] {'zl','x'}, dimensions={0} | all-to-all | bytes 2097152 | tf_op jit(solution)/shard_map/all_to_all | solution.py:154
  120.2 2.2 %collective-permute-start.2 = (bf16[8,32,2048]{2,1,0:T(8,128)(2,1)S(1)}, bf16[8,32,2048]{2,1,0:T(8,128)(2,1)S(1)}, u32[]{:S(2)}, u32[]{:S(2)}) collective-permute-start(bf16[8,32,2048]{2,1,0:T(8,128)(2,1)S(1)} %all_to_all.41), channel_id=1, source_target_pairs={{0,1},{1,0},{2,3},{3,2},{4,5},{5,4},{6,7},{7,6},{8,9},{9,8},{10,11... | collective-permute-start | bytes 3145736 | tf_op jit(solution)/shard_map/ppermute | solution.py:155
  122.3 0.1 fusion.86
  122.4 2.5 %collective-permute-done.2 = bf16[8,32,2048]{2,1,0:T(8,128)(2,1)S(1)} collective-permute-done((bf16[8,32,2048]{2,1,0:T(8,128)(2,1)S(1)}, bf16[8,32,2048]{2,1,0:T(8,128)(2,1)S(1)}, u32[]{:S(2)}, u32[]{:S(2)}) %collective-permute-start.2) | collective-permute-done | bytes 1048608 | tf_op jit(solution)/shard_map/ppermute | solution.py:155
  125.0 0.9 fusion.87
  125.9 0.8 copy-done.2
  126.7 1.5 fusion.15
  128.1 3.5 %fusion.11 = f32[256,2048]{1,0:T(8,128)S(1)} fusion(bf16[2,384,2048]{2,1,0:T(8,128)(2,1)} %param.23, bf16[2,2048,384]{2,1,0:T(8,128)(2,1)} %param.22, bf16[128,2048]{1,0:T(8,128)(2,1)} %bitcast.111, bf16[128,2048]{1,0:T(8,128)(2,1)S(1)} %bitcast.107, f32[256,384]{1,0:T(8,128)} %fusion.15), kind=kOutput, calls=%fused_computation.15 | convolution fusion | flops 807993344 | bytes 6684672 | tf_op jit(solution)/shard_map/dot_general | solution.py:167
  131.7 3.7 %fusion.9 = f32[256,384]{1,0:T(8,128)} fusion(bf16[2,2048,384]{2,1,0:T(8,128)(2,1)} %param.21, bf16[128,2048]{1,0:T(8,128)(2,1)} %bitcast.108, bf16[128,2048]{1,0:T(8,128)(2,1)S(1)} %bitcast.104), kind=kOutput, calls=%fused_computation.13 | convolution fusion | flops 404750336 | bytes 3014656 | tf_op jit(solution)/shard_map/dot_general | solution.py:164
  135.4 4.8 %fusion.5 = f32[256,2048]{1,0:T(8,128)} fusion(bf16[2,384,2048]{2,1,0:T(8,128)(2,1)} %param.23, bf16[2,2048,384]{2,1,0:T(8,128)(2,1)} %param.22, bf16[128,2048]{1,0:T(8,128)(2,1)} %bitcast.109, bf16[128,2048]{1,0:T(8,128)(2,1)S(1)} %bitcast.105, f32[256,384]{1,0:T(8,128)} %fusion.9), kind=kOutput, calls=%fused_computation.9 | convolution fusion | flops 807993344 | bytes 6684672 | tf_op jit(solution)/shard_map/dot_general | solution.py:167
  140.2 1.3 slice.191
  141.5 0.1 pad_maximum_fusion.2
  141.6 2.2 %collective-permute-start.3 = (bf16[8,32,2048]{2,1,0:T(8,128)(2,1)S(1)}, bf16[8,32,2048]{2,1,0:T(8,128)(2,1)S(1)}, u32[]{:S(2)}, u32[]{:S(2)}) collective-permute-start(bf16[8,32,2048]{2,1,0:T(8,128)(2,1)S(1)} %pad_maximum_fusion.2), channel_id=1, source_target_pairs={{0,1},{1,0},{2,3},{3,2},{4,5},{5,4},{6,7},{7,6},{8,9},{9,8},{10,11... | collective-permute-start | bytes 3145736 | tf_op jit(solution)/shard_map/ppermute | solution.py:173
  143.8 2.5 %collective-permute-done.3 = bf16[8,32,2048]{2,1,0:T(8,128)(2,1)S(1)} collective-permute-done((bf16[8,32,2048]{2,1,0:T(8,128)(2,1)S(1)}, bf16[8,32,2048]{2,1,0:T(8,128)(2,1)S(1)}, u32[]{:S(2)}, u32[]{:S(2)}) %collective-permute-start.3) | collective-permute-done | bytes 1048608 | tf_op jit(solution)/shard_map/ppermute | solution.py:173
  146.3 1.3 fusion.4
  147.6 5.3 %all-to-all-start.6 = ((bf16[8,32,2048]{2,1,0:T(8,128)(2,1)}), bf16[8,32,2048]{2,1,0:T(8,128)(2,1)S(1)}, u32[]{:S(2)}, u32[]{:S(2)}) async-start(bf16[8,32,2048]{2,1,0:T(8,128)(2,1)} %fusion.4), calls=%async_computation.6 | async-start | bytes 2097152 | tf_op jit(solution)/shard_map/all_to_all | solution.py:175
  152.9 0.1 fusion.54
  153.0 14.1 %all-to-all-done.6 = bf16[8,32,2048]{2,1,0:T(8,128)(2,1)S(1)} async-done(((bf16[8,32,2048]{2,1,0:T(8,128)(2,1)}), bf16[8,32,2048]{2,1,0:T(8,128)(2,1)S(1)}, u32[]{:S(2)}, u32[]{:S(2)}) %all-to-all-start.6) | async-done | bytes 1048608 | tf_op jit(solution)/shard_map/all_to_all | solution.py:175
  167.1 0.3 fusion.89
  167.4 0.3 fusion.2
  167.8 26.8 %all_to_all.42 = bf16[8,8,2048]{2,1,0:T(8,128)(2,1)S(1)} all-to-all(bf16[8,8,2048]{2,1,0:T(8,128)(2,1)S(1)} %fusion.2), channel_id=1, replica_groups=mesh['zh'=8,'zl'=2,'x'=4,'head'=8,'pair'=2] {'zh'}, dimensions={0} | all-to-all | bytes 524288 | tf_op jit(solution)/shard_map/all_to_all | solution.py:182
  194.6 0.6 add_convert_fusion
  (50 shorter events, 1.1 us)
Async XLA Ops:
  0.0 48.1 %copy-start = (bf16[128,128]{1,0:T(8,128)(2,1)S(1)}, bf16[128,128]{1,0:T(8,128)(2,1)}, u32[]{:S(2)}) copy-start(bf16[128,128]{1,0:T(8,128)(2,1)} %param.12) | copy-start | bytes 98308
  21.2 43.2 %copy-start.5 = (s32[16,8]{0,1:T(8,128)S(1)}, s32[16,8]{0,1:T(8,128)}, u32[]{:S(2)}) copy-start(s32[16,8]{0,1:T(8,128)} %param.19) | copy-start | bytes 1540
  21.2 43.4 %copy-start.6 = (f32[16,8]{0,1:T(8,128)S(1)}, f32[16,8]{0,1:T(8,128)}, u32[]{:S(2)}) copy-start(f32[16,8]{0,1:T(8,128)} %param.20) | copy-start | bytes 1540
  21.2 21.5 %all-to-all-start.1 = ((bf16[16,32,128]{2,1,0:T(8,128)(2,1)}), bf16[16,32,128]{2,1,0:T(8,128)(2,1)S(1)}, u32[]{:S(2)}, u32[]{:S(2)}) async-start(bf16[16,32,128]{2,1,0:T(8,128)(2,1)} %broadcast_in_dim.45), calls=%async_computation.1 | async-start | bytes 262144 | tf_op jit(solution)/shard_map/all_to_all | solution.py:25
  29.3 27.1 %collective-permute-start.1 = (bf16[128,2048]{1,0:T(8,128)(2,1)}, bf16[128,2048]{1,0:T(8,128)(2,1)S(1)}, u32[]{:S(2)}, u32[]{:S(2)}) collective-permute-start(bf16[128,2048]{1,0:T(8,128)(2,1)} %param.17), channel_id=1, source_target_pairs={{0,1},{1,0},{2,3},{3,2},{4,5},{5,4},{6,7},{7,6},{8,9},{9,8},{10,11... | collective-permute-start | bytes 1572872 | tf_op jit(solution)/shard_map/ppermute | solution.py:106
  31.2 45.7 %copy-start.3 = (bf16[8,2048]{1,0:T(8,128)(2,1)S(1)}, bf16[8,2048]{1,0:T(8,128)(2,1)}, u32[]{:S(2)}) copy-start(bf16[8,2048]{1,0:T(8,128)(2,1)} %param.15) | copy-start | bytes 98308
  42.8 34.3 %copy-start.4 = (f32[2048]{0:T(1024)S(1)}, f32[2048]{0:T(1024)}, u32[]{:S(2)}) copy-start(f32[2048]{0:T(1024)} %param.18) | copy-start | bytes 24580
  43.4 8.7 %all-to-all-start.2 = ((bf16[4,32,128]{2,1,0:T(8,128)(2,1)}), bf16[4,32,128]{2,1,0:T(8,128)(2,1)S(1)}, u32[]{:S(2)}, u32[]{:S(2)}) async-start(bf16[4,32,128]{2,1,0:T(8,128)(2,1)} %pad_maximum_fusion.9), calls=%async_computation.2 | async-start | bytes 65536 | tf_op jit(solution)/shard_map/all_to_all | solution.py:41
  53.1 3.2 %collective-permute-start = (bf16[64,128]{1,0:T(8,128)(2,1)S(1)}, bf16[64,128]{1,0:T(8,128)(2,1)S(1)}, u32[]{:S(2)}, u32[]{:S(2)}) collective-permute-start(bf16[64,128]{1,0:T(8,128)(2,1)S(1)} %select_bitcast_fusion), channel_id=1, source_target_pairs={{0,1},{1,0},{2,3},{3,2},{4,5},{5,4},{6,7},{7,6},{8,9},{9,8},{10,11... | collective-permute-start | bytes 49160 | tf_op jit(solution)/shard_map/ppermute | solution.py:125
  57.3 19.6 %all-to-all-start.3 = ((bf16[8,8,2048]{2,1,0:T(8,128)(2,1)}), bf16[8,8,2048]{2,1,0:T(8,128)(2,1)S(1)}, u32[]{:S(2)}, u32[]{:S(2)}) async-start(bf16[8,8,2048]{2,1,0:T(8,128)(2,1)} %fusion.3), calls=%async_computation.3 | async-start | bytes 524288 | tf_op jit(solution)/shard_map/all_to_all | solution.py:130
  78.0 23.8 %all-to-all-start.4 = ((bf16[8,8,2176]{2,1,0:T(8,128)(2,1)}), bf16[8,8,2176]{2,1,0:T(8,128)(2,1)S(1)}, u32[]{:S(2)}, u32[]{:S(2)}) async-start(bf16[8,8,2176]{2,1,0:T(8,128)(2,1)} %broadcast_in_dim.48), calls=%async_computation.4 | async-start | bytes 557056 | tf_op jit(solution)/shard_map/all_to_all | solution.py:25
  120.2 6.5 %copy-start.7 = (bf16[2,2048,384]{2,1,0:T(8,128)(2,1)S(1)}, bf16[2,2048,384]{2,1,0:T(8,128)(2,1)}, u32[]{:S(2)}) copy-start(bf16[2,2048,384]{2,1,0:T(8,128)(2,1)} %param.21) | copy-start | bytes 9437188
  120.2 4.8 %collective-permute-start.2 = (bf16[8,32,2048]{2,1,0:T(8,128)(2,1)S(1)}, bf16[8,32,2048]{2,1,0:T(8,128)(2,1)S(1)}, u32[]{:S(2)}, u32[]{:S(2)}) collective-permute-start(bf16[8,32,2048]{2,1,0:T(8,128)(2,1)S(1)} %all_to_all.41), channel_id=1, source_target_pairs={{0,1},{1,0},{2,3},{3,2},{4,5},{5,4},{6,7},{7,6},{8,9},{9,8},{10,11... | collective-permute-start | bytes 3145736 | tf_op jit(solution)/shard_map/ppermute | solution.py:155
  125.8 0.8 copy-start.2
  131.6 12.2 %copy-start.1 = (f32[256,2048]{1,0:T(8,128)}, f32[256,2048]{1,0:T(8,128)S(1)}, u32[]{:S(2)}) copy-start(f32[256,2048]{1,0:T(8,128)S(1)} %fusion.11) | copy-start | bytes 6291460
  141.6 4.7 %slice-start.1 = ((f32[256,2048]{1,0:T(8,128)}), f32[128,2048]{1,0:T(8,128)S(1)}, s32[]{:S(2)}) async-start(f32[256,2048]{1,0:T(8,128)} %fusion.5), calls=%async_computation.9 | async-start | bytes 2097152 | tf_op jit(solution)/shard_map/slice | solution.py:169
  141.6 4.7 %collective-permute-start.3 = (bf16[8,32,2048]{2,1,0:T(8,128)(2,1)S(1)}, bf16[8,32,2048]{2,1,0:T(8,128)(2,1)S(1)}, u32[]{:S(2)}, u32[]{:S(2)}) collective-permute-start(bf16[8,32,2048]{2,1,0:T(8,128)(2,1)S(1)} %pad_maximum_fusion.2), channel_id=1, source_target_pairs={{0,1},{1,0},{2,3},{3,2},{4,5},{5,4},{6,7},{7,6},{8,9},{9,8},{10,11... | collective-permute-start | bytes 3145736 | tf_op jit(solution)/shard_map/ppermute | solution.py:173
  143.8 2.5 %slice-start = ((f32[256,2048]{1,0:T(8,128)}), f32[128,2048]{1,0:T(8,128)S(1)}, s32[]{:S(2)}) async-start(f32[256,2048]{1,0:T(8,128)} %copy-done.1), calls=%async_computation.8 | async-start | bytes 2097152 | tf_op jit(solution)/shard_map/slice | solution.py:169
  147.6 19.5 %all-to-all-start.6 = ((bf16[8,32,2048]{2,1,0:T(8,128)(2,1)}), bf16[8,32,2048]{2,1,0:T(8,128)(2,1)S(1)}, u32[]{:S(2)}, u32[]{:S(2)}) async-start(bf16[8,32,2048]{2,1,0:T(8,128)(2,1)} %fusion.4), calls=%async_computation.6 | async-start | bytes 2097152 | tf_op jit(solution)/shard_map/all_to_all | solution.py:175

commit v3 on v2

--- a/solution.py
+++ b/solution.py
@@ -1,13 +1,15 @@
 import jax
 import jax.numpy as jnp
 from jax import lax
+from jax.experimental import pallas as pl
+from jax.experimental.pallas import tpu as pltpu
 from jax.sharding import Mesh
 from jax.sharding import PartitionSpec as P
 
 LANES = 128
 CAP = 2
 Z = ("zh", "zl")
-NEAR = ("zl", "x")
+NEAR = ("zl", "x", "pair")
 SEQ = ("zh", "zl", "x")
 SEQ_HEAD_PAIR = ("zh", "zl", "x", "head", "pair")
 SEQ_HEAD = ("zh", "zl", "x", "head")
@@ -85,6 +87,59 @@
     return fills.astype(jnp.bfloat16), added
 
 
+def expert_kernel(core, rows, g0, u0, d0, g1, u1, d1, out, gate_all, up_all, down_all, sems):
+    mine = core[0]
+    half = g0.shape[2]
+    copies = []
+    for place, (parts, whole) in enumerate(
+        (((g0, g1), gate_all), ((u0, u1), up_all), ((d0, d1), down_all))
+    ):
+        for index, part in enumerate(parts):
+            span = pl.ds(index * half, half)
+            view = whole.at[span, :] if whole is down_all else whole.at[:, span]
+            copies.append(pltpu.make_async_copy(part.at[mine], view, sems.at[place, index]))
+    for copy in copies:
+        copy.start()
+    values = rows[...]
+    copies[0].wait()
+    copies[1].wait()
+    gate_part = jnp.dot(values, gate_all[...], preferred_element_type=jnp.float32)
+    copies[2].wait()
+    copies[3].wait()
+    up_part = jnp.dot(values, up_all[...], preferred_element_type=jnp.float32)
+    hidden = (gate_part / (1.0 + jnp.exp(-gate_part)) * up_part).astype(jnp.bfloat16)
+    copies[4].wait()
+    copies[5].wait()
+    result = jnp.dot(hidden, down_all[...], preferred_element_type=jnp.float32)
+    out[...] = result.astype(out.dtype)
+
+
+def expert(core, rows, own_parts, other_parts):
+    _, width, half = own_parts[0].shape
+    parts = [
+        pltpu.with_memory_space_constraint(part, pltpu.HBM) for part in (*own_parts, *other_parts)
+    ]
+    in_place = [pl.BlockSpec(memory_space=pl.ANY)] * 6
+    return pl.pallas_call(
+        expert_kernel,
+        out_shape=jax.ShapeDtypeStruct(rows.shape, jnp.bfloat16),
+        in_specs=[
+            pl.BlockSpec(memory_space=pltpu.SMEM),
+            pl.BlockSpec(memory_space=pltpu.VMEM),
+            *in_place,
+        ],
+        out_specs=pl.BlockSpec(memory_space=pltpu.VMEM),
+        scratch_shapes=[
+            pltpu.VMEM((width, 2 * half), jnp.bfloat16),
+            pltpu.VMEM((width, 2 * half), jnp.bfloat16),
+            pltpu.VMEM((2 * half, width), jnp.bfloat16),
+            pltpu.SemaphoreType.DMA((3, 2)),
+        ],
+        compiler_params=pltpu.CompilerParams(vmem_limit_bytes=24 * 1024 * 1024),
+        name="expert",
+    )(core.reshape(1).astype(jnp.int32), rows, *parts)
+
+
 def body(
     query_rows,
     all_head_keys,
@@ -104,11 +159,14 @@
     heads = lax.axis_size("head")
     core = lax.axis_index("pair")
     other_weight = lax.ppermute(out_weight, "pair", SWAP)
+    other_parts = [lax.ppermute(part, "pair", SWAP) for part in (w_gate, w_up, w_down)]
 
     local_state = jnp.einsum(
         "tz,td->zd", all_head_keys, value_rows, preferred_element_type=jnp.float32
     )
-    previous = entering_state(local_state)
+    previous, other_parts[0] = lax.optimization_barrier(
+        (entering_state(local_state), other_parts[0])
+    )
     causal = jnp.arange(length)[:, None] >= jnp.arange(length)[None, :]
     scores = jnp.where(
         causal,
@@ -140,39 +198,17 @@
     packed = packed.reshape(blocks * block_rows, -1)
     routing = packed[:, model_width : model_width + 3 * top].astype(jnp.float32)
     weights = routing[:, top : 2 * top] + routing[:, 2 * top :]
-    experts_here = w_gate.shape[0]
     near = lax.axis_size(NEAR)
     fills, added = slot_matrices(
-        routing[:, :top],
-        weights,
-        lax.axis_index("zh") * near * experts_here,
-        near * experts_here,
-        block_rows,
+        routing[:, :top], weights, lax.axis_index("zh") * near, near, block_rows
     )
     slots = jnp.dot(fills, packed[:, :model_width], preferred_element_type=jnp.float32)
     slots = slots.astype(jnp.bfloat16).reshape(near, -1, model_width)
-    own = lax.all_to_all(slots, NEAR, 0, 0, tiled=True)
-    other = lax.ppermute(own, "pair", SWAP)
-
-    per_expert = blocks * CAP
-    for_own, for_other = [], []
-    for expert in range(experts_here):
-        span = slice(expert * per_expert, (expert + 1) * per_expert)
-        rows = jnp.concatenate(
-            [own[:, span].reshape(-1, model_width), other[:, span].reshape(-1, model_width)]
-        )
-        gate_part = jnp.dot(rows, w_gate[expert], preferred_element_type=jnp.float32)
-        up_part = jnp.dot(rows, w_up[expert], preferred_element_type=jnp.float32)
-        activated = (jax.nn.silu(gate_part) * up_part).astype(jnp.bfloat16)
-        result = jnp.dot(activated, w_down[expert], preferred_element_type=jnp.float32)
-        half = near * per_expert
-        for_own.append(result[:half].reshape(near, per_expert, model_width))
-        for_other.append(
-            result[half:].astype(jnp.bfloat16).reshape(near, per_expert, model_width)
-        )
-    from_other = lax.ppermute(jnp.concatenate(for_other, axis=1), "pair", SWAP)
-    expert_out = jnp.concatenate(for_own, axis=1) + from_other.astype(jnp.float32)
-    returned = lax.all_to_all(expert_out.astype(jnp.bfloat16), NEAR, 0, 0, tiled=True)
+    slots, *other_parts[1:] = lax.optimization_barrier((slots, *other_parts[1:]))
+    rows = lax.all_to_all(slots, NEAR, 0, 0, tiled=True).reshape(-1, model_width)
+
+    expert_out = expert(core, rows, (w_gate, w_up, w_down), other_parts).reshape(slots.shape)
+    returned = lax.all_to_all(expert_out, NEAR, 0, 0, tiled=True)
     returned = returned.reshape(-1, model_width)
 
     high, low = two_terms(added)

time: 196 us -> 185 us (0.944)
  the two profiles are of different devices: /device:TPU:2 before, /device:TPU:7 now
where the time goes in v3:
time: 185 us; the launch traced here: 184 us
  blocking collectives  84.6 us (46%)
  starting transfers between devices  40.3 us (22%)
  waiting for transfers between devices  29.8 us (16%)
  local copies, waits for them, and re-layouts  7.82 us (4%)
  other arithmetic  7.79 us (4%)
  matrix products  7.53 us (4%)
  Pallas kernels  5.41 us (3%)
    all_to_all x1, blocking collectives, body(): sums = lax.all_to_all(sums, 'zh', 0, 0, tiled=True)  24.8 us
    all_to_all x1, blocking collectives, body(): lax.all_to_all(slots, NEAR, 0, 0, tiled=True).reshape(-1, model_width)  23.1 us
    all_to_all x2, waiting for transfers between devices, to_each(): return lax.all_to_all(copies, axis, 0, 0, tiled=True)  21.2 us
    all_to_all x1, blocking collectives, body(): returned = lax.all_to_all(expert_out, NEAR, 0, 0, tiled=True)  19 us
    all_to_all x1, blocking collectives, entering_state(): parts = lax.all_to_all(parts, 'x', 0, 0, tiled=True).astype(jnp.float32)  17.7 us
    all_to_all x2, starting transfers between devices, to_each(): return lax.all_to_all(copies, axis, 0, 0, tiled=True)  10.8 us
    ppermute x3, starting transfers between devices, body(): lax.ppermute(part, 'pair', SWAP)  7.18 us
    all_to_all x1, waiting for transfers between devices, body(): partial_rows = lax.all_to_all(partial_rows, 'head', 0, 0, tiled=True)  7.11 us
  transfers between devices with their start and end apart: 9, of which 4 were waited for; matrix products, arithmetic and copies ran while one was open for 10% of the time, Pallas kernels for 0%

profile of v3, /device:TPU:7, one launch (start us, length us, event | category | flops | bytes accessed | tf_op | source)
XLA Modules:
  0.0 183.6 jit_solution(4858734850160314934)
XLA Ops:
  0.0 2.9 %collective-permute-start = (bf16[2,2048,384]{2,1,0:T(8,128)(2,1)}, bf16[2,2048,384]{2,1,0:T(8,128)(2,1)}, u32[]{:S(2)}, u32[]{:S(2)}) collective-permute-start(bf16[2,2048,384]{2,1,0:T(8,128)(2,1)} %g0.1), channel_id=1, source_target_pairs={{0,1},{1,0},{2,3},{3,2},{4,5},{5,4},{6,7},{7,6},{8,9},{9,8},{10,11... | collective-permute-start | bytes 9437192 | tf_op jit(solution)/shard_map/ppermute | solution.py:162
  2.9 1.0 convolution_convert_fusion.1
  3.9 17.7 %all_to_all.40 = bf16[4,32,128]{2,1,0:T(8,128)(2,1)S(1)} all-to-all(bf16[4,32,128]{2,1,0:T(8,128)(2,1)S(1)} %bitcast.72), channel_id=1, replica_groups=mesh['zh'=8,'zl'=2,'x'=4,'head'=8,'pair'=2] {'x'}, dimensions={0} | all-to-all | bytes 65536 | tf_op jit(solution)/shard_map/all_to_all | solution.py:35
  21.5 0.7 broadcast_in_dim.45
  22.2 7.4 %all-to-all-start.1 = ((bf16[16,32,128]{2,1,0:T(8,128)(2,1)}), bf16[16,32,128]{2,1,0:T(8,128)(2,1)S(1)}, u32[]{:S(2)}, u32[]{:S(2)}) async-start(bf16[16,32,128]{2,1,0:T(8,128)(2,1)} %broadcast_in_dim.45), calls=%async_computation.1 | async-start | bytes 262144 | tf_op jit(solution)/shard_map/all_to_all | solution.py:27
  29.7 3.6 %collective-permute-start.2 = (bf16[128,2048]{1,0:T(8,128)(2,1)}, bf16[128,2048]{1,0:T(8,128)(2,1)}, u32[]{:S(2)}, u32[]{:S(2)}) collective-permute-start(bf16[128,2048]{1,0:T(8,128)(2,1)} %param.17), channel_id=1, source_target_pairs={{0,1},{1,0},{2,3},{3,2},{4,5},{5,4},{6,7},{7,6},{8,9},{9,8},{10,11... | collective-permute-start | bytes 1572872 | tf_op jit(solution)/shard_map/ppermute | solution.py:161
  33.3 8.3 %all-to-all-done.1 = bf16[16,32,128]{2,1,0:T(8,128)(2,1)S(1)} async-done(((bf16[16,32,128]{2,1,0:T(8,128)(2,1)}), bf16[16,32,128]{2,1,0:T(8,128)(2,1)S(1)}, u32[]{:S(2)}, u32[]{:S(2)}) %all-to-all-start.1) | async-done | bytes 131104 | tf_op jit(solution)/shard_map/all_to_all | solution.py:27
  41.6 0.1 select_reduce_fusion
  41.8 0.6 pad_maximum_fusion
  42.4 5.0 %all-to-all-start.2 = ((bf16[4,32,128]{2,1,0:T(8,128)(2,1)}), bf16[4,32,128]{2,1,0:T(8,128)(2,1)S(1)}, u32[]{:S(2)}, u32[]{:S(2)}) async-start(bf16[4,32,128]{2,1,0:T(8,128)(2,1)} %pad_maximum_fusion), calls=%async_computation.2 | async-start | bytes 65536 | tf_op jit(solution)/shard_map/all_to_all | solution.py:43
  47.4 1.0 fusion.6
  48.5 1.4 all-to-all-done.2
  49.9 0.2 multiply_reduce_fusion.1
  50.2 0.7 multiply_convert_fusion.1
  50.9 6.8 %collective-permute-start.1 = (bf16[64,128]{1,0:T(8,128)(2,1)S(1)}, bf16[64,128]{1,0:T(8,128)(2,1)S(1)}, u32[]{:S(2)}, u32[]{:S(2)}) collective-permute-start(bf16[64,128]{1,0:T(8,128)(2,1)S(1)} %select_bitcast_fusion), channel_id=1, source_target_pairs={{0,1},{1,0},{2,3},{3,2},{4,5},{5,4},{6,7},{7,6},{8,9},{9,8},{10,11... | collective-permute-start | bytes 49160 | tf_op jit(solution)/shard_map/ppermute | solution.py:183
  57.7 1.3 fusion.29
  59.0 2.0 %fusion.3 = bf16[8,8,2048]{2,1,0:T(8,128)(2,1)} fusion(f32[64,2048]{1,0:T(8,128)S(1)} %fusion.29, bf16[64,128]{1,0:T(8,128)(2,1)S(1)} %collective-permute-done.1, bf16[128,2048]{1,0:T(8,128)(2,1)} %collective-permute-done.2), kind=kOutput, calls=%fused_computation.7 | convolution fusion | flops 33816576 | bytes 1327104 | tf_op jit(solution)/shard_map/dot_general | solution.py:184
  61.0 6.8 %all-to-all-start.3 = ((bf16[8,8,2048]{2,1,0:T(8,128)(2,1)}), bf16[8,8,2048]{2,1,0:T(8,128)(2,1)S(1)}, u32[]{:S(2)}, u32[]{:S(2)}) async-start(bf16[8,8,2048]{2,1,0:T(8,128)(2,1)} %fusion.3), calls=%async_computation.3 | async-start | bytes 524288 | tf_op jit(solution)/shard_map/all_to_all | solution.py:188
  67.8 2.2 %collective-permute-start.3 = (bf16[2,2048,384]{2,1,0:T(8,128)(2,1)S(1)}, bf16[2,2048,384]{2,1,0:T(8,128)(2,1)}, u32[]{:S(2)}, u32[]{:S(2)}) collective-permute-start(bf16[2,2048,384]{2,1,0:T(8,128)(2,1)S(1)} %copy-done.1), channel_id=1, source_target_pairs={{0,1},{1,0},{2,3},{3,2},{4,5},{5,4},{6,7},{7,6},{8,9},{9,8},{10,11... | collective-permute-start | bytes 9437192 | tf_op jit(solution)/shard_map/ppermute | solution.py:162
  70.0 2.1 %collective-permute-start.4 = (bf16[2,384,2048]{2,1,0:T(8,128)(2,1)}, bf16[2,384,2048]{2,1,0:T(8,128)(2,1)}, u32[]{:S(2)}, u32[]{:S(2)}) collective-permute-start(bf16[2,384,2048]{2,1,0:T(8,128)(2,1)} %d0.1), channel_id=1, source_target_pairs={{0,1},{1,0},{2,3},{3,2},{4,5},{5,4},{6,7},{7,6},{8,9},{9,8},{10,11... | collective-permute-start | bytes 9437192 | tf_op jit(solution)/shard_map/ppermute | solution.py:162
  72.5 0.6 fusion.38
  73.0 7.1 %all-to-all-done.3 = bf16[8,8,2048]{2,1,0:T(8,128)(2,1)S(1)} async-done(((bf16[8,8,2048]{2,1,0:T(8,128)(2,1)}), bf16[8,8,2048]{2,1,0:T(8,128)(2,1)S(1)}, u32[]{:S(2)}, u32[]{:S(2)}) %all-to-all-start.3) | async-done | bytes 262176 | tf_op jit(solution)/shard_map/all_to_all | solution.py:188
  80.2 0.1 multiply_reduce_fusion
  80.4 0.1 multiply_convert_fusion
  80.4 0.8 concatenate.3
  81.2 0.7 broadcast_in_dim.48
  81.9 3.4 %all-to-all-start.4 = ((bf16[8,8,2176]{2,1,0:T(8,128)(2,1)}), bf16[8,8,2176]{2,1,0:T(8,128)(2,1)S(1)}, u32[]{:S(2)}, u32[]{:S(2)}) async-start(bf16[8,8,2176]{2,1,0:T(8,128)(2,1)} %broadcast_in_dim.48), calls=%async_computation.4 | async-start | bytes 557056 | tf_op jit(solution)/shard_map/all_to_all | solution.py:27
  85.4 0.6 and_select_fusion.2
  85.9 0.6 copy-done.5
  86.5 0.6 eq.95
  87.1 1.3 eq.96
  88.4 0.6 add_convert_fusion.1
  89.0 1.3 broadcast_compare_fusion
  90.4 12.9 %all-to-all-done.4 = bf16[8,8,2176]{2,1,0:T(8,128)(2,1)S(1)} async-done(((bf16[8,8,2176]{2,1,0:T(8,128)(2,1)}), bf16[8,8,2176]{2,1,0:T(8,128)(2,1)S(1)}, u32[]{:S(2)}, u32[]{:S(2)}) %all-to-all-start.4) | async-done | bytes 278560 | tf_op jit(solution)/shard_map/all_to_all | solution.py:27
  103.3 0.7 slice_bitcast_fusion
  104.0 1.4 copy.22
  105.4 1.4 copy.23
  106.8 0.8 fusion.12
  107.6 0.9 convolution_select_fusion.1
  108.5 0.8 fusion.9
  109.3 0.4 convolution_convert_fusion
  109.7 23.1 %all_to_all.41 = bf16[16,16,2048]{2,1,0:T(8,128)(2,1)S(1)} all-to-all(bf16[16,16,2048]{2,1,0:T(8,128)(2,1)S(1)} %bitcast.67), channel_id=1, replica_groups=mesh['zh'=8,'zl'=2,'x'=4,'head'=8,'pair'=2] {'zl','x','pair'}, dimensions={0} | all-to-all | bytes 2097152 | tf_op jit(solution)/shard_map/all_to_all | solution.py:208
  132.8 5.4 %expert.1 = bf16[256,2048]{1,0:T(8,128)(2,1)S(1)} custom-call(s32[1]{0:T(128)} %bitcast.11.core, bf16[256,2048]{1,0:T(8,128)(2,1)S(1)} %bitcast.65, bf16[2,2048,384]{2,1,0:T(8,128)(2,1)} %g0.1, bf16[2,2048,384]{2,1,0:T(8,128)(2,1)} %u0.1, bf16[2,384,2048]{2,1,0:T(8,128)(2,1)} %d0.1, bf16[2,2048,384]{2,1,0:T(8,128)(2,1)} %collective-permute-done.g1, ...), custom_call_target="tpu_custom_call" | custom-call | tf_op jit(solution)/shard_map/expert/pallas_call | solution.py:123
  138.2 19.0 %all_to_all.42 = bf16[16,16,2048]{2,1,0:T(8,128)(2,1)S(1)} all-to-all(bf16[16,16,2048]{2,1,0:T(8,128)(2,1)S(1)} %bitcast.66), channel_id=1, replica_groups=mesh['zh'=8,'zl'=2,'x'=4,'head'=8,'pair'=2] {'zl','x','pair'}, dimensions={0} | all-to-all | bytes 2097152 | tf_op jit(solution)/shard_map/all_to_all | solution.py:211
  157.3 0.4 convolution_bitcast_fusion.1
  157.7 0.4 fusion.4
  158.1 24.8 %all_to_all.43 = bf16[8,8,2048]{2,1,0:T(8,128)(2,1)S(1)} all-to-all(bf16[8,8,2048]{2,1,0:T(8,128)(2,1)S(1)} %fusion.4), channel_id=1, replica_groups=mesh['zh'=8,'zl'=2,'x'=4,'head'=8,'pair'=2] {'zh'}, dimensions={0} | all-to-all | bytes 524288 | tf_op jit(solution)/shard_map/all_to_all | solution.py:218
  183.0 0.6 add_convert_fusion
  (41 shorter events, 0.5 us)
Async XLA Ops:
  0.0 47.4 %copy-start = (bf16[128,128]{1,0:T(8,128)(2,1)S(1)}, bf16[128,128]{1,0:T(8,128)(2,1)}, u32[]{:S(2)}) copy-start(bf16[128,128]{1,0:T(8,128)(2,1)} %param.12) | copy-start | bytes 98308
  0.0 67.8 %copy-start.1 = (bf16[2,2048,384]{2,1,0:T(8,128)(2,1)S(1)}, bf16[2,2048,384]{2,1,0:T(8,128)(2,1)}, u32[]{:S(2)}) copy-start(bf16[2,2048,384]{2,1,0:T(8,128)(2,1)} %u0.1) | copy-start | bytes 9437188
  0.0 72.1 %copy-start.7 = (s32[16,8]{0,1:T(8,128)S(1)}, s32[16,8]{0,1:T(8,128)}, u32[]{:S(2)}) copy-start(s32[16,8]{0,1:T(8,128)} %param.19) | copy-start | bytes 1540
  0.0 72.3 %copy-start.8 = (f32[16,8]{0,1:T(8,128)S(1)}, f32[16,8]{0,1:T(8,128)}, u32[]{:S(2)}) copy-start(f32[16,8]{0,1:T(8,128)} %param.20) | copy-start | bytes 1540
  0.0 80.2 %copy-start.2 = (bf16[8,2048]{1,0:T(8,128)(2,1)S(1)}, bf16[8,2048]{1,0:T(8,128)(2,1)}, u32[]{:S(2)}) copy-start(bf16[8,2048]{1,0:T(8,128)(2,1)} %param.15) | copy-start | bytes 98308
  0.0 80.3 %copy-start.4 = (f32[2048]{0:T(1024)S(1)}, f32[2048]{0:T(1024)}, u32[]{:S(2)}) copy-start(f32[2048]{0:T(1024)} %param.18) | copy-start | bytes 24580
  0.0 49.9 %collective-permute-start = (bf16[2,2048,384]{2,1,0:T(8,128)(2,1)}, bf16[2,2048,384]{2,1,0:T(8,128)(2,1)}, u32[]{:S(2)}, u32[]{:S(2)}) collective-permute-start(bf16[2,2048,384]{2,1,0:T(8,128)(2,1)} %g0.1), channel_id=1, source_target_pairs={{0,1},{1,0},{2,3},{3,2},{4,5},{5,4},{6,7},{7,6},{8,9},{9,8},{10,11... | collective-permute-start | bytes 9437192 | tf_op jit(solution)/shard_map/ppermute | solution.py:162
  22.2 19.4 %all-to-all-start.1 = ((bf16[16,32,128]{2,1,0:T(8,128)(2,1)}), bf16[16,32,128]{2,1,0:T(8,128)(2,1)S(1)}, u32[]{:S(2)}, u32[]{:S(2)}) async-start(bf16[16,32,128]{2,1,0:T(8,128)(2,1)} %broadcast_in_dim.45), calls=%async_computation.1 | async-start | bytes 262144 | tf_op jit(solution)/shard_map/all_to_all | solution.py:27
  29.7 29.3 %collective-permute-start.2 = (bf16[128,2048]{1,0:T(8,128)(2,1)}, bf16[128,2048]{1,0:T(8,128)(2,1)}, u32[]{:S(2)}, u32[]{:S(2)}) collective-permute-start(bf16[128,2048]{1,0:T(8,128)(2,1)} %param.17), channel_id=1, source_target_pairs={{0,1},{1,0},{2,3},{3,2},{4,5},{5,4},{6,7},{7,6},{8,9},{9,8},{10,11... | collective-permute-start | bytes 1572872 | tf_op jit(solution)/shard_map/ppermute | solution.py:161
  42.4 7.5 %all-to-all-start.2 = ((bf16[4,32,128]{2,1,0:T(8,128)(2,1)}), bf16[4,32,128]{2,1,0:T(8,128)(2,1)S(1)}, u32[]{:S(2)}, u32[]{:S(2)}) async-start(bf16[4,32,128]{2,1,0:T(8,128)(2,1)} %pad_maximum_fusion), calls=%async_computation.2 | async-start | bytes 65536 | tf_op jit(solution)/shard_map/all_to_all | solution.py:43
  50.9 8.1 %collective-permute-start.1 = (bf16[64,128]{1,0:T(8,128)(2,1)S(1)}, bf16[64,128]{1,0:T(8,128)(2,1)S(1)}, u32[]{:S(2)}, u32[]{:S(2)}) collective-permute-start(bf16[64,128]{1,0:T(8,128)(2,1)S(1)} %select_bitcast_fusion), channel_id=1, source_target_pairs={{0,1},{1,0},{2,3},{3,2},{4,5},{5,4},{6,7},{7,6},{8,9},{9,8},{10,11... | collective-permute-start | bytes 49160 | tf_op jit(solution)/shard_map/ppermute | solution.py:183
  61.0 19.2 %all-to-all-start.3 = ((bf16[8,8,2048]{2,1,0:T(8,128)(2,1)}), bf16[8,8,2048]{2,1,0:T(8,128)(2,1)S(1)}, u32[]{:S(2)}, u32[]{:S(2)}) async-start(bf16[8,8,2048]{2,1,0:T(8,128)(2,1)} %fusion.3), calls=%async_computation.3 | async-start | bytes 524288 | tf_op jit(solution)/shard_map/all_to_all | solution.py:188
  67.8 41.9 %collective-permute-start.3 = (bf16[2,2048,384]{2,1,0:T(8,128)(2,1)S(1)}, bf16[2,2048,384]{2,1,0:T(8,128)(2,1)}, u32[]{:S(2)}, u32[]{:S(2)}) collective-permute-start(bf16[2,2048,384]{2,1,0:T(8,128)(2,1)S(1)} %copy-done.1), channel_id=1, source_target_pairs={{0,1},{1,0},{2,3},{3,2},{4,5},{5,4},{6,7},{7,6},{8,9},{9,8},{10,11... | collective-permute-start | bytes 9437192 | tf_op jit(solution)/shard_map/ppermute | solution.py:162
  70.0 39.7 %collective-permute-start.4 = (bf16[2,384,2048]{2,1,0:T(8,128)(2,1)}, bf16[2,384,2048]{2,1,0:T(8,128)(2,1)}, u32[]{:S(2)}, u32[]{:S(2)}) collective-permute-start(bf16[2,384,2048]{2,1,0:T(8,128)(2,1)} %d0.1), channel_id=1, source_target_pairs={{0,1},{1,0},{2,3},{3,2},{4,5},{5,4},{6,7},{7,6},{8,9},{9,8},{10,11... | collective-permute-start | bytes 9437192 | tf_op jit(solution)/shard_map/ppermute | solution.py:162
  81.9 21.4 %all-to-all-start.4 = ((bf16[8,8,2176]{2,1,0:T(8,128)(2,1)}), bf16[8,8,2176]{2,1,0:T(8,128)(2,1)S(1)}, u32[]{:S(2)}, u32[]{:S(2)}) async-start(bf16[8,8,2176]{2,1,0:T(8,128)(2,1)} %broadcast_in_dim.48), calls=%async_computation.4 | async-start | bytes 557056 | tf_op jit(solution)/shard_map/all_to_all | solution.py:27
  85.9 0.6 copy-start.5
  88.4 0.6 copy-start.9
  132.8 24.5 %copy-start.3 = (pred[16,64]{1,0:T(8,128)(4,1)S(1)}, pred[16,64]{1,0:T(8,128)(4,1)}, u32[]{:S(2)}) copy-start(pred[16,64]{1,0:T(8,128)(4,1)} %broadcast_compare_fusion) | copy-start | bytes 3076
  132.8 24.5 %copy-start.6 = (f32[16]{0:T(128)S(1)}, f32[16]{0:T(128)}, u32[]{:S(2)}) copy-start(f32[16]{0:T(128)} %copy-done.5) | copy-start | bytes 196

commit v4 on v3

--- a/solution.py
+++ b/solution.py
@@ -1,3 +1,5 @@
+import functools
+
 import jax
 import jax.numpy as jnp
 from jax import lax
@@ -5,6 +7,7 @@
 from jax.experimental.pallas import tpu as pltpu
 from jax.sharding import Mesh
 from jax.sharding import PartitionSpec as P
+
 
 LANES = 128
 CAP = 2
@@ -22,9 +25,8 @@
     return values * lax.rsqrt(mean_sq + EPSILON) * gain_vec
 
 
-def to_each(shard, axis):
-    copies = jnp.broadcast_to(shard[None], (lax.axis_size(axis), *shard.shape))
-    return lax.all_to_all(copies, axis, 0, 0, tiled=True)
+def copied(shard, axis):
+    return jnp.broadcast_to(shard[None], (lax.axis_size(axis), *shard.shape))
 
 
 def entering_state(local_state):
@@ -32,8 +34,10 @@
     across = lax.axis_size("x")
     along = lax.axis_size(Z)
     parts = local_state.astype(jnp.bfloat16).reshape(across, rows // across, width)
-    parts = lax.all_to_all(parts, "x", 0, 0, tiled=True).astype(jnp.float32)
-    totals = to_each(jnp.sum(parts, axis=0).astype(jnp.bfloat16), Z).astype(jnp.float32)
+    parts = lax.all_to_all(parts, "x", 0, 0, tiled=True)
+    parts = parts.astype(jnp.float32)
+    copies = copied(jnp.sum(parts, axis=0).astype(jnp.bfloat16), Z)
+    totals = lax.all_to_all(copies, Z, 0, 0, tiled=True).astype(jnp.float32)
     passed = (jnp.arange(along) < lax.axis_index(Z))[:, None, None]
     running = jnp.sum(jnp.where(passed, totals, 0.0), axis=0)
     entering = []
@@ -64,27 +68,61 @@
     return jnp.concatenate([rows, tail], axis=1)
 
 
-def slot_matrices(ids, weights, first, experts, block_rows):
-    count = ids.shape[0]
+def slot_kernel(first, packed, slots, high, low, *, block_rows, top):
+    count, width = packed.shape[0], slots.shape[1]
     blocks = count // block_rows
-    wanted = first + jnp.arange(experts, dtype=jnp.int32)
-    named = wanted.astype(jnp.float32)[:, None, None] == ids.T[None]
-    chosen = jnp.sum(named.astype(jnp.float32), axis=1)
-    weight = jnp.sum(jnp.where(named, weights.T[None], 0.0), axis=1)
-    row = jnp.arange(count)
-    same_block = row[:, None] // block_rows == row[None, :] // block_rows
-    ahead = (same_block & (row[:, None] < row[None, :])).astype(jnp.bfloat16)
-    rank = jnp.dot(chosen.astype(jnp.bfloat16), ahead, preferred_element_type=jnp.float32)
-    code = jnp.where(chosen > 0.0, rank, -1.0)
-    per_expert = blocks * CAP
-    slot = jnp.arange(per_expert)
-    in_block = slot[:, None] // CAP == row[None, :] // block_rows
-    slot_rank = (slot % CAP).astype(jnp.float32)
-    fills = in_block[None] & (code[:, None, :] == slot_rank[None, :, None])
-    fills = fills.reshape(experts * per_expert, count)
-    added = jnp.broadcast_to(weight[:, None, :], (experts, per_expert, count))
-    added = jnp.where(fills, added.reshape(fills.shape), 0.0)
-    return fills.astype(jnp.bfloat16), added
+    shape = (count, slots.shape[0])
+    routing = packed[:, width:].astype(jnp.float32)
+    slot = lax.broadcasted_iota(jnp.int32, shape, 1)
+    row = lax.broadcasted_iota(jnp.int32, shape, 0)
+    wanted = (first[0] + slot // (blocks * CAP)).astype(jnp.float32)
+    chosen = jnp.zeros(shape, jnp.float32)
+    weight = jnp.zeros(shape, jnp.float32)
+    for k in range(top):
+        named = routing[:, k : k + 1] == wanted
+        value = routing[:, top + k : top + k + 1] + routing[:, 2 * top + k : 2 * top + k + 1]
+        chosen = jnp.where(named, 1.0, chosen)
+        weight = jnp.where(named, value, weight)
+    to_row = lax.broadcasted_iota(jnp.int32, (count, count), 0)
+    from_row = lax.broadcasted_iota(jnp.int32, (count, count), 1)
+    ahead = (to_row // block_rows == from_row // block_rows) & (from_row < to_row)
+    rank = jnp.dot(
+        jnp.where(ahead, 1.0, 0.0).astype(jnp.bfloat16),
+        chosen.astype(jnp.bfloat16),
+        preferred_element_type=jnp.float32,
+    )
+    fills = (
+        (chosen > 0.0)
+        & (rank == (slot % CAP).astype(jnp.float32))
+        & (slot // CAP % blocks == row // block_rows)
+    )
+    picks = jnp.where(fills, 1.0, 0.0).astype(jnp.bfloat16)
+    slots[...] = lax.dot_general(
+        picks, packed[:, :width], (((0,), (0,)), ((), ())), preferred_element_type=jnp.float32
+    ).astype(slots.dtype)
+    added = jnp.where(fills, weight, 0.0)
+    rounded = added.astype(jnp.bfloat16)
+    high[...] = rounded
+    low[...] = (added - rounded.astype(jnp.float32)).astype(jnp.bfloat16)
+
+
+def sorted_into_slots(packed, first, experts, block_rows, top):
+    count = packed.shape[0]
+    slots = experts * (count // block_rows) * CAP
+    width = packed.shape[1] - LANES
+    on_chip = pl.BlockSpec(memory_space=pltpu.VMEM)
+    return pl.pallas_call(
+        functools.partial(slot_kernel, block_rows=block_rows, top=top),
+        out_shape=(
+            jax.ShapeDtypeStruct((slots, width), jnp.bfloat16),
+            jax.ShapeDtypeStruct((count, slots), jnp.bfloat16),
+            jax.ShapeDtypeStruct((count, slots), jnp.bfloat16),
+        ),
+        in_specs=[pl.BlockSpec(memory_space=pltpu.SMEM), on_chip],
+        out_specs=(on_chip, on_chip, on_chip),
+        compiler_params=pltpu.CompilerParams(vmem_limit_bytes=12 * 1024 * 1024),
+        name="slots",
+    )(first.reshape(1).astype(jnp.int32), packed)
 
 
 def expert_kernel(core, rows, g0, u0, d0, g1, u1, d1, out, gate_all, up_all, down_all, sems):
@@ -140,7 +178,7 @@
     )(core.reshape(1).astype(jnp.int32), rows, *parts)
 
 
-def body(
+def layer(
     query_rows,
     all_head_keys,
     value_rows,
@@ -159,14 +197,11 @@
     heads = lax.axis_size("head")
     core = lax.axis_index("pair")
     other_weight = lax.ppermute(out_weight, "pair", SWAP)
-    other_parts = [lax.ppermute(part, "pair", SWAP) for part in (w_gate, w_up, w_down)]
-
     local_state = jnp.einsum(
         "tz,td->zd", all_head_keys, value_rows, preferred_element_type=jnp.float32
     )
-    previous, other_parts[0] = lax.optimization_barrier(
-        (entering_state(local_state), other_parts[0])
-    )
+    other_gate = lax.ppermute(w_gate, "pair", SWAP)
+    previous, other_gate = lax.optimization_barrier((entering_state(local_state), other_gate))
     causal = jnp.arange(length)[:, None] >= jnp.arange(length)[None, :]
     scores = jnp.where(
         causal,
@@ -185,35 +220,35 @@
         taken, other_weight, preferred_element_type=jnp.float32
     )
     partial_rows = partial_rows.astype(jnp.bfloat16).reshape(heads, block_rows, model_width)
+    other_up = lax.ppermute(w_up, "pair", SWAP)
+    other_down = lax.ppermute(w_down, "pair", SWAP)
     partial_rows = lax.all_to_all(partial_rows, "head", 0, 0, tiled=True)
     projected = jnp.sum(partial_rows.astype(jnp.float32), axis=0)
     residual = stream.astype(jnp.float32) + projected
     moe_input = rms_scale(residual, moe_gain).astype(jnp.bfloat16)
 
-    top = routes.shape[1]
     my_routes = lax.dynamic_slice_in_dim(routes, core * block_rows, block_rows, 0)
     my_weights = lax.dynamic_slice_in_dim(gate_weights, core * block_rows, block_rows, 0)
-    packed = to_each(with_routing(moe_input, my_routes, my_weights), "zh")
+    packed = copied(with_routing(moe_input, my_routes, my_weights), "zh")
+    packed = lax.all_to_all(packed, "zh", 0, 0, tiled=True)
     blocks = packed.shape[0]
     packed = packed.reshape(blocks * block_rows, -1)
-    routing = packed[:, model_width : model_width + 3 * top].astype(jnp.float32)
-    weights = routing[:, top : 2 * top] + routing[:, 2 * top :]
     near = lax.axis_size(NEAR)
-    fills, added = slot_matrices(
-        routing[:, :top], weights, lax.axis_index("zh") * near, near, block_rows
-    )
-    slots = jnp.dot(fills, packed[:, :model_width], preferred_element_type=jnp.float32)
-    slots = slots.astype(jnp.bfloat16).reshape(near, -1, model_width)
-    slots, *other_parts[1:] = lax.optimization_barrier((slots, *other_parts[1:]))
+    slots, high, low = sorted_into_slots(
+        packed, lax.axis_index("zh") * near, near, block_rows, routes.shape[1]
+    )
+    slots = slots.reshape(near, -1, model_width)
+    slots, other_up, other_down = lax.optimization_barrier((slots, other_up, other_down))
     rows = lax.all_to_all(slots, NEAR, 0, 0, tiled=True).reshape(-1, model_width)
 
-    expert_out = expert(core, rows, (w_gate, w_up, w_down), other_parts).reshape(slots.shape)
+    expert_out = expert(
+        core, rows, (w_gate, w_up, w_down), (other_gate, other_up, other_down)
+    ).reshape(slots.shape)
     returned = lax.all_to_all(expert_out, NEAR, 0, 0, tiled=True)
     returned = returned.reshape(-1, model_width)
 
-    high, low = two_terms(added)
-    sums = jnp.einsum("sr,sd->rd", high, returned, preferred_element_type=jnp.float32)
-    sums = sums + jnp.einsum("sr,sd->rd", low, returned, preferred_element_type=jnp.float32)
+    sums = jnp.dot(high, returned, preferred_element_type=jnp.float32)
+    sums = sums + jnp.dot(low, returned, preferred_element_type=jnp.float32)
     sums = sums.astype(jnp.bfloat16).reshape(blocks, block_rows, model_width)
     sums = lax.all_to_all(sums, "zh", 0, 0, tiled=True)
     combined = jnp.sum(sums.astype(jnp.float32), axis=0)
@@ -240,5 +275,5 @@
         P(SEQ, "pair", None),
     )
     return jax.shard_map(
-        body, mesh=split, in_specs=placed, out_specs=P(SEQ_HEAD_PAIR, None), check_vma=False
-    )
+        layer, mesh=split, in_specs=placed, out_specs=P(SEQ_HEAD_PAIR, None), check_vma=False
+    )

time: 185 us -> 179 us (0.968)
  local copies, waits for them, and re-layouts: 7.82 us -> 3.16 us
  waiting for transfers between devices: 29.8 us -> 34 us
  other arithmetic: 7.79 us -> 3.65 us
    all_to_all x3, waiting for transfers between devices: 28.4 us -> 32.6 us  [the longest x1 18.4 us: layer(): packed = lax.all_to_all(packed, 'zh', 0, 0, tiled=True)]
    transpose x2 -> x0, local copies, waits for them, and re-layouts: 2.84 us -> none  [the longest x1 1.42 us: slot_matrices(): named = wanted.astype(jnp.float32)[:, None, None] == ids.T[None]]
    eq x2 -> x0, local copies, waits for them, and re-layouts: 1.91 us -> none  [slot_matrices(): fills = in_block[None] & (code[:, None, :] == slot_rank[None, :, None])]
    dot_general x9 -> x7, matrix products: 7.53 us -> 6.06 us  [the longest x1 1.96 us: layer(): jnp.dot(taken, other_weight, preferred_element_type=jnp.float32)]
  transfers between devices with their start and end apart: 9 -> 9, of which waited for: 4 -> 4; matrix products, arithmetic and copies ran while one was open for 10% -> 7% of each run, Pallas kernels for 0% -> 0%
where the time goes in v4:
time: 179 us; the launch traced here: 178 us
  blocking collectives  83.6 us (47%)
  starting transfers between devices  40.7 us (23%)
  waiting for transfers between devices  34 us (19%)
  Pallas kernels  6.17 us (3%)
  matrix products  6.06 us (3%)
  other arithmetic  3.65 us (2%)
  local copies, waits for them, and re-layouts  3.16 us (2%)
    all_to_all x1, blocking collectives, layer(): sums = lax.all_to_all(sums, 'zh', 0, 0, tiled=True)  23.8 us
    all_to_all x1, blocking collectives, layer(): lax.all_to_all(slots, NEAR, 0, 0, tiled=True).reshape(-1, model_width)  23 us
    all_to_all x1, blocking collectives, layer(): returned = lax.all_to_all(expert_out, NEAR, 0, 0, tiled=True)  19.1 us
    all_to_all x1, waiting for transfers between devices, layer(): packed = lax.all_to_all(packed, 'zh', 0, 0, tiled=True)  18.4 us
    all_to_all x1, blocking collectives, entering_state(): parts = lax.all_to_all(parts, 'x', 0, 0, tiled=True)  17.7 us
    all_to_all x1, waiting for transfers between devices, layer(): partial_rows = lax.all_to_all(partial_rows, 'head', 0, 0, tiled=True)  10.2 us
    all_to_all x1, starting transfers between devices, entering_state(): totals = lax.all_to_all(copies, Z, 0, 0, tiled=True).astype(jnp.float32)  7.43 us
    all_to_all x1, starting transfers between devices, layer(): partial_rows = lax.all_to_all(partial_rows, 'head', 0, 0, tiled=True)  6.82 us
  transfers between devices with their start and end apart: 9, of which 4 were waited for; matrix products, arithmetic and copies ran while one was open for 7% of the time, Pallas kernels for 0%

profile of v4, /device:TPU:7, one launch (start us, length us, event | category | flops | bytes accessed | tf_op | source)
XLA Modules:
  0.0 177.6 jit_solution(5626272522010503966)
XLA Ops:
  0.0 0.0 copy-start
  0.0 0.0 copy-start.3
  0.0 2.7 %collective-permute-start = (bf16[2,2048,384]{2,1,0:T(8,128)(2,1)}, bf16[2,2048,384]{2,1,0:T(8,128)(2,1)S(1)}, u32[]{:S(2)}, u32[]{:S(2)}) collective-permute-start(bf16[2,2048,384]{2,1,0:T(8,128)(2,1)} %g0.1), channel_id=1, source_target_pairs={{0,1},{1,0},{2,3},{3,2},{4,5},{5,4},{6,7},{7,6},{8,9},{9,8},{10,11... | collective-permute-start | bytes 9437192 | tf_op jit(solution)/shard_map/ppermute | solution.py:203
  2.7 1.0 convolution_convert_fusion
  3.7 17.7 %all_to_all.40 = bf16[4,32,128]{2,1,0:T(8,128)(2,1)S(1)} all-to-all(bf16[4,32,128]{2,1,0:T(8,128)(2,1)S(1)} %bitcast.56), channel_id=1, replica_groups=mesh['zh'=8,'zl'=2,'x'=4,'head'=8,'pair'=2] {'x'}, dimensions={0} | all-to-all | bytes 65536 | tf_op jit(solution)/shard_map/all_to_all | solution.py:37
  21.4 0.7 broadcast_in_dim.24
  22.1 7.4 %all-to-all-start.1 = ((bf16[16,32,128]{2,1,0:T(8,128)(2,1)}), bf16[16,32,128]{2,1,0:T(8,128)(2,1)S(1)}, u32[]{:S(2)}, u32[]{:S(2)}) async-start(bf16[16,32,128]{2,1,0:T(8,128)(2,1)} %broadcast_in_dim.24), calls=%async_computation.1 | async-start | bytes 262144 | tf_op jit(solution)/shard_map/all_to_all | solution.py:40
  29.5 3.6 %collective-permute-start.2 = (bf16[128,2048]{1,0:T(8,128)(2,1)}, bf16[128,2048]{1,0:T(8,128)(2,1)}, u32[]{:S(2)}, u32[]{:S(2)}) collective-permute-start(bf16[128,2048]{1,0:T(8,128)(2,1)} %param.17), channel_id=1, source_target_pairs={{0,1},{1,0},{2,3},{3,2},{4,5},{5,4},{6,7},{7,6},{8,9},{9,8},{10,11... | collective-permute-start | bytes 1572872 | tf_op jit(solution)/shard_map/ppermute | solution.py:199
  33.1 1.9 %collective-permute-start.3 = (bf16[2,2048,384]{2,1,0:T(8,128)(2,1)}, bf16[2,2048,384]{2,1,0:T(8,128)(2,1)}, u32[]{:S(2)}, u32[]{:S(2)}) collective-permute-start(bf16[2,2048,384]{2,1,0:T(8,128)(2,1)} %u0.1), channel_id=1, source_target_pairs={{0,1},{1,0},{2,3},{3,2},{4,5},{5,4},{6,7},{7,6},{8,9},{9,8},{10,11... | collective-permute-start | bytes 9437192 | tf_op jit(solution)/shard_map/ppermute | solution.py:223
  35.1 2.4 %collective-permute-start.4 = (bf16[2,384,2048]{2,1,0:T(8,128)(2,1)}, bf16[2,384,2048]{2,1,0:T(8,128)(2,1)}, u32[]{:S(2)}, u32[]{:S(2)}) collective-permute-start(bf16[2,384,2048]{2,1,0:T(8,128)(2,1)} %d0.1), channel_id=1, source_target_pairs={{0,1},{1,0},{2,3},{3,2},{4,5},{5,4},{6,7},{7,6},{8,9},{9,8},{10,11... | collective-permute-start | bytes 9437192 | tf_op jit(solution)/shard_map/ppermute | solution.py:224
  37.5 4.0 %all-to-all-done.1 = bf16[16,32,128]{2,1,0:T(8,128)(2,1)S(1)} async-done(((bf16[16,32,128]{2,1,0:T(8,128)(2,1)}), bf16[16,32,128]{2,1,0:T(8,128)(2,1)S(1)}, u32[]{:S(2)}, u32[]{:S(2)}) %all-to-all-start.1) | async-done | bytes 131104 | tf_op jit(solution)/shard_map/all_to_all | solution.py:40
  41.5 0.1 select_reduce_fusion
  41.6 0.6 pad_maximum_fusion
  42.2 5.0 %all-to-all-start.2 = ((bf16[4,32,128]{2,1,0:T(8,128)(2,1)}), bf16[4,32,128]{2,1,0:T(8,128)(2,1)S(1)}, u32[]{:S(2)}, u32[]{:S(2)}) async-start(bf16[4,32,128]{2,1,0:T(8,128)(2,1)} %pad_maximum_fusion), calls=%async_computation.2 | async-start | bytes 65536 | tf_op jit(solution)/shard_map/all_to_all | solution.py:47
  47.3 1.0 fusion.5
  48.3 1.4 all-to-all-done.2
  49.8 0.0 collective-permute-done.g1
  49.8 0.2 multiply_reduce_fusion.1
  50.0 0.8 multiply_convert_fusion.1
  50.8 6.8 %collective-permute-start.1 = (bf16[64,128]{1,0:T(8,128)(2,1)S(1)}, bf16[64,128]{1,0:T(8,128)(2,1)S(1)}, u32[]{:S(2)}, u32[]{:S(2)}) collective-permute-start(bf16[64,128]{1,0:T(8,128)(2,1)S(1)} %select_bitcast_fusion), channel_id=1, source_target_pairs={{0,1},{1,0},{2,3},{3,2},{4,5},{5,4},{6,7},{7,6},{8,9},{9,8},{10,11... | collective-permute-start | bytes 49160 | tf_op jit(solution)/shard_map/ppermute | solution.py:218
  57.6 1.3 fusion.8
  58.9 0.0 collective-permute-done.2
  58.9 0.0 collective-permute-done.1
  58.9 2.0 %fusion.3 = bf16[8,8,2048]{2,1,0:T(8,128)(2,1)} fusion(f32[64,2048]{1,0:T(8,128)S(1)} %fusion.8, bf16[64,128]{1,0:T(8,128)(2,1)S(1)} %collective-permute-done.1, bf16[128,2048]{1,0:T(8,128)(2,1)} %collective-permute-done.2), kind=kOutput, calls=%fused_computation.5 | convolution fusion | flops 33816576 | bytes 1327104 | tf_op jit(solution)/shard_map/dot_general | solution.py:219
  60.9 6.8 %all-to-all-start.3 = ((bf16[8,8,2048]{2,1,0:T(8,128)(2,1)}), bf16[8,8,2048]{2,1,0:T(8,128)(2,1)S(1)}, u32[]{:S(2)}, u32[]{:S(2)}) async-start(bf16[8,8,2048]{2,1,0:T(8,128)(2,1)} %fusion.3), calls=%async_computation.3 | async-start | bytes 524288 | tf_op jit(solution)/shard_map/all_to_all | solution.py:225
  67.7 0.1 constant_dynamic-slice_fusion.1
  67.8 0.1 copy.17
  67.8 0.6 convert_element_type.78
  68.4 0.8 constant_dynamic-slice_fusion
  69.2 0.1 copy.18
  69.3 0.6 fusion.15
  69.8 10.2 %all-to-all-done.3 = bf16[8,8,2048]{2,1,0:T(8,128)(2,1)S(1)} async-done(((bf16[8,8,2048]{2,1,0:T(8,128)(2,1)}), bf16[8,8,2048]{2,1,0:T(8,128)(2,1)S(1)}, u32[]{:S(2)}, u32[]{:S(2)}) %all-to-all-start.3) | async-done | bytes 262176 | tf_op jit(solution)/shard_map/all_to_all | solution.py:225
  80.1 0.1 multiply_reduce_fusion
  80.2 0.1 multiply_convert_fusion
  80.3 0.8 concatenate.3
  81.1 0.7 broadcast_in_dim.43
  81.8 4.0 %all-to-all-start.4 = ((bf16[8,8,2176]{2,1,0:T(8,128)(2,1)}), bf16[8,8,2176]{2,1,0:T(8,128)(2,1)S(1)}, u32[]{:S(2)}, u32[]{:S(2)}) async-start(bf16[8,8,2176]{2,1,0:T(8,128)(2,1)} %broadcast_in_dim.43), calls=%async_computation.4 | async-start | bytes 557056 | tf_op jit(solution)/shard_map/all_to_all | solution.py:233
  85.8 18.4 %all-to-all-done.4 = bf16[8,8,2176]{2,1,0:T(8,128)(2,1)S(1)} async-done(((bf16[8,8,2176]{2,1,0:T(8,128)(2,1)}), bf16[8,8,2176]{2,1,0:T(8,128)(2,1)S(1)}, u32[]{:S(2)}, u32[]{:S(2)}) %all-to-all-start.4) | async-done | bytes 278560 | tf_op jit(solution)/shard_map/all_to_all | solution.py:233
  104.2 0.8 slots.1
  105.0 0.0 collective-permute-done.3.u1
  105.0 0.0 collective-permute-done.4.d1
  105.0 23.0 %all_to_all.41 = bf16[16,16,2048]{2,1,0:T(8,128)(2,1)S(1)} all-to-all(bf16[16,16,2048]{2,1,0:T(8,128)(2,1)S(1)} %bitcast.51), channel_id=1, replica_groups=mesh['zh'=8,'zl'=2,'x'=4,'head'=8,'pair'=2] {'zl','x','pair'}, dimensions={0} | all-to-all | bytes 2097152 | tf_op jit(solution)/shard_map/all_to_all | solution.py:242
  128.0 5.4 %expert.1 = bf16[256,2048]{1,0:T(8,128)(2,1)S(1)} custom-call(s32[1]{0:T(128)} %bitcast.10.core, bf16[256,2048]{1,0:T(8,128)(2,1)S(1)} %bitcast.48, bf16[2,2048,384]{2,1,0:T(8,128)(2,1)} %g0.1, bf16[2,2048,384]{2,1,0:T(8,128)(2,1)} %u0.1, bf16[2,384,2048]{2,1,0:T(8,128)(2,1)} %d0.1, bf16[2,2048,384]{2,1,0:T(8,128)(2,1)} %copy-done.1, ...), custom_call_target="tpu_custom_call" | custom-call | tf_op jit(solution)/shard_map/expert/pallas_call | solution.py:161
  133.4 19.1 %all_to_all.42 = bf16[16,16,2048]{2,1,0:T(8,128)(2,1)S(1)} all-to-all(bf16[16,16,2048]{2,1,0:T(8,128)(2,1)S(1)} %bitcast.49), channel_id=1, replica_groups=mesh['zh'=8,'zl'=2,'x'=4,'head'=8,'pair'=2] {'zl','x','pair'}, dimensions={0} | all-to-all | bytes 2097152 | tf_op jit(solution)/shard_map/all_to_all | solution.py:247
  152.5 0.3 fusion.19
  152.8 0.3 fusion.2
  153.1 23.8 %all_to_all.43 = bf16[8,8,2048]{2,1,0:T(8,128)(2,1)S(1)} all-to-all(bf16[8,8,2048]{2,1,0:T(8,128)(2,1)S(1)} %fusion.2), channel_id=1, replica_groups=mesh['zh'=8,'zl'=2,'x'=4,'head'=8,'pair'=2] {'zh'}, dimensions={0} | all-to-all | bytes 524288 | tf_op jit(solution)/shard_map/all_to_all | solution.py:253
  177.0 0.6 add_convert_fusion
  (18 shorter events, 0.1 us)
Async XLA Ops:
  0.0 47.3 %copy-start = (bf16[128,128]{1,0:T(8,128)(2,1)S(1)}, bf16[128,128]{1,0:T(8,128)(2,1)}, u32[]{:S(2)}) copy-start(bf16[128,128]{1,0:T(8,128)(2,1)} %param.12) | copy-start | bytes 98308
  0.0 67.7 %copy-start.4 = (s32[16,8]{0,1:T(8,128)S(1)}, s32[16,8]{0,1:T(8,128)}, u32[]{:S(2)}) copy-start(s32[16,8]{0,1:T(8,128)} %param.19) | copy-start | bytes 1540
  0.0 80.1 %copy-start.2 = (bf16[8,2048]{1,0:T(8,128)(2,1)S(1)}, bf16[8,2048]{1,0:T(8,128)(2,1)}, u32[]{:S(2)}) copy-start(bf16[8,2048]{1,0:T(8,128)(2,1)} %param.15) | copy-start | bytes 98308
  0.0 80.2 %copy-start.3 = (f32[2048]{0:T(1024)S(1)}, f32[2048]{0:T(1024)}, u32[]{:S(2)}) copy-start(f32[2048]{0:T(1024)} %param.18) | copy-start | bytes 24580
  0.0 49.7 %collective-permute-start = (bf16[2,2048,384]{2,1,0:T(8,128)(2,1)}, bf16[2,2048,384]{2,1,0:T(8,128)(2,1)S(1)}, u32[]{:S(2)}, u32[]{:S(2)}) collective-permute-start(bf16[2,2048,384]{2,1,0:T(8,128)(2,1)} %g0.1), channel_id=1, source_target_pairs={{0,1},{1,0},{2,3},{3,2},{4,5},{5,4},{6,7},{7,6},{8,9},{9,8},{10,11... | collective-permute-start | bytes 9437192 | tf_op jit(solution)/shard_map/ppermute | solution.py:203
  22.1 19.4 %all-to-all-start.1 = ((bf16[16,32,128]{2,1,0:T(8,128)(2,1)}), bf16[16,32,128]{2,1,0:T(8,128)(2,1)S(1)}, u32[]{:S(2)}, u32[]{:S(2)}) async-start(bf16[16,32,128]{2,1,0:T(8,128)(2,1)} %broadcast_in_dim.24), calls=%async_computation.1 | async-start | bytes 262144 | tf_op jit(solution)/shard_map/all_to_all | solution.py:40
  29.5 29.4 %collective-permute-start.2 = (bf16[128,2048]{1,0:T(8,128)(2,1)}, bf16[128,2048]{1,0:T(8,128)(2,1)}, u32[]{:S(2)}, u32[]{:S(2)}) collective-permute-start(bf16[128,2048]{1,0:T(8,128)(2,1)} %param.17), channel_id=1, source_target_pairs={{0,1},{1,0},{2,3},{3,2},{4,5},{5,4},{6,7},{7,6},{8,9},{9,8},{10,11... | collective-permute-start | bytes 1572872 | tf_op jit(solution)/shard_map/ppermute | solution.py:199
  33.1 71.8 %collective-permute-start.3 = (bf16[2,2048,384]{2,1,0:T(8,128)(2,1)}, bf16[2,2048,384]{2,1,0:T(8,128)(2,1)}, u32[]{:S(2)}, u32[]{:S(2)}) collective-permute-start(bf16[2,2048,384]{2,1,0:T(8,128)(2,1)} %u0.1), channel_id=1, source_target_pairs={{0,1},{1,0},{2,3},{3,2},{4,5},{5,4},{6,7},{7,6},{8,9},{9,8},{10,11... | collective-permute-start | bytes 9437192 | tf_op jit(solution)/shard_map/ppermute | solution.py:223
  35.1 69.9 %collective-permute-start.4 = (bf16[2,384,2048]{2,1,0:T(8,128)(2,1)}, bf16[2,384,2048]{2,1,0:T(8,128)(2,1)}, u32[]{:S(2)}, u32[]{:S(2)}) collective-permute-start(bf16[2,384,2048]{2,1,0:T(8,128)(2,1)} %d0.1), channel_id=1, source_target_pairs={{0,1},{1,0},{2,3},{3,2},{4,5},{5,4},{6,7},{7,6},{8,9},{9,8},{10,11... | collective-permute-start | bytes 9437192 | tf_op jit(solution)/shard_map/ppermute | solution.py:224
  42.2 7.5 %all-to-all-start.2 = ((bf16[4,32,128]{2,1,0:T(8,128)(2,1)}), bf16[4,32,128]{2,1,0:T(8,128)(2,1)S(1)}, u32[]{:S(2)}, u32[]{:S(2)}) async-start(bf16[4,32,128]{2,1,0:T(8,128)(2,1)} %pad_maximum_fusion), calls=%async_computation.2 | async-start | bytes 65536 | tf_op jit(solution)/shard_map/all_to_all | solution.py:47
  49.8 78.3 %copy-start.1 = (bf16[2,2048,384]{2,1,0:T(8,128)(2,1)}, bf16[2,2048,384]{2,1,0:T(8,128)(2,1)S(1)}, u32[]{:S(2)}) copy-start(bf16[2,2048,384]{2,1,0:T(8,128)(2,1)S(1)} %collective-permute-done.g1) | copy-start | bytes 9437188
  50.8 8.1 %collective-permute-start.1 = (bf16[64,128]{1,0:T(8,128)(2,1)S(1)}, bf16[64,128]{1,0:T(8,128)(2,1)S(1)}, u32[]{:S(2)}, u32[]{:S(2)}) collective-permute-start(bf16[64,128]{1,0:T(8,128)(2,1)S(1)} %select_bitcast_fusion), channel_id=1, source_target_pairs={{0,1},{1,0},{2,3},{3,2},{4,5},{5,4},{6,7},{7,6},{8,9},{9,8},{10,11... | collective-permute-start | bytes 49160 | tf_op jit(solution)/shard_map/ppermute | solution.py:218
  60.9 19.2 %all-to-all-start.3 = ((bf16[8,8,2048]{2,1,0:T(8,128)(2,1)}), bf16[8,8,2048]{2,1,0:T(8,128)(2,1)S(1)}, u32[]{:S(2)}, u32[]{:S(2)}) async-start(bf16[8,8,2048]{2,1,0:T(8,128)(2,1)} %fusion.3), calls=%async_computation.3 | async-start | bytes 524288 | tf_op jit(solution)/shard_map/all_to_all | solution.py:225
  81.8 22.4 %all-to-all-start.4 = ((bf16[8,8,2176]{2,1,0:T(8,128)(2,1)}), bf16[8,8,2176]{2,1,0:T(8,128)(2,1)S(1)}, u32[]{:S(2)}, u32[]{:S(2)}) async-start(bf16[8,8,2176]{2,1,0:T(8,128)(2,1)} %broadcast_in_dim.43), calls=%async_computation.4 | async-start | bytes 557056 | tf_op jit(solution)/shard_map/all_to_all | solution.py:233

commit v5 on v4

--- a/solution.py
+++ b/solution.py
@@ -44,8 +44,10 @@
     for place in range(across):
         entering.append(running.astype(jnp.bfloat16))
         running = running + parts[place]
-    back = lax.all_to_all(jnp.stack(entering), "x", 0, 0, tiled=True)
-    return back.reshape(rows, width)
+    entering = jnp.repeat(jnp.stack(entering), lax.axis_size("pair"), axis=0)
+    back = lax.all_to_all(entering, ("x", "pair"), 0, 0, tiled=True)
+    back = back.reshape(across, lax.axis_size("pair"), rows // across, width)
+    return jnp.moveaxis(back, 1, 0).reshape(-1, rows, width)
 
 
 def two_terms(values):
@@ -53,19 +55,110 @@
     return high.astype(jnp.bfloat16), (values - high).astype(jnp.bfloat16)
 
 
-def with_routing(rows, expert_ids, weights):
+def routing_tail(expert_ids, weights):
     count, top = expert_ids.shape
     high, low = two_terms(weights)
-    tail = jnp.concatenate(
-        [
-            expert_ids.astype(jnp.bfloat16),
-            high,
-            low,
-            jnp.zeros((count, LANES - 3 * top), jnp.bfloat16),
+    unused = jnp.zeros((count, LANES - 3 * top), jnp.bfloat16)
+    return jnp.concatenate([expert_ids.astype(jnp.bfloat16), high, low, unused], axis=1)
+
+
+def attend_kernel(
+    core, q0, q1, parts0, parts1, gain1, w1, entering, gain_in, w_in, out, gain0, w0, sems, *, block_rows
+):
+    copies = [
+        pltpu.make_async_copy(gain_in, gain0, sems.at[0]),
+        pltpu.make_async_copy(w_in, w0, sems.at[1]),
+    ]
+    for copy in copies:
+        copy.start()
+    mine = core[0]
+    count, length = q0.shape[0], parts0.shape[1]
+    place = lax.broadcasted_iota(jnp.int32, (count, length), 0)
+    row = place // block_rows * 2 * block_rows + mine * block_rows + place % block_rows
+    causal = lax.broadcasted_iota(jnp.int32, (count, length), 1) <= row
+
+    def scaled(q, parts, state):
+        scores = lax.dot_general(
+            q[...], parts[1], (((1,), (1,)), ((), ())), preferred_element_type=jnp.float32
+        )
+        scores = jnp.where(causal, scores, 0.0)
+        high = scores.astype(jnp.bfloat16)
+        low = (scores - high.astype(jnp.float32)).astype(jnp.bfloat16)
+        mixed = jnp.dot(high, parts[2], preferred_element_type=jnp.float32)
+        mixed = mixed + jnp.dot(low, parts[2], preferred_element_type=jnp.float32)
+        mixed = mixed + jnp.dot(q[...], state, preferred_element_type=jnp.float32)
+        return rms_scale(mixed, jnp.ones_like(gain1[...]))
+
+    rows1 = (scaled(q1, parts1, entering[1 - mine]) * gain1[...]).astype(jnp.bfloat16)
+    rows0 = scaled(q0, parts0, entering[mine])
+    for copy in copies:
+        copy.wait()
+    rows0 = (rows0 * gain0[...]).astype(jnp.bfloat16)
+    total = jnp.dot(rows1, w1[...], preferred_element_type=jnp.float32)
+    total = total + jnp.dot(rows0, w0[...], preferred_element_type=jnp.float32)
+    out[...] = total.astype(out.dtype)
+
+
+def attended(core, own, other, entering, block_rows):
+    def kept(parts):
+        by_core = parts[0].reshape(-1, 2, block_rows, parts.shape[2])
+        return jnp.where(core == 0, by_core[:, 0], by_core[:, 1]).reshape(-1, parts.shape[2])
+
+    own_parts, own_gain, own_weight = own
+    other_parts, other_gain, other_weight = other
+    query = kept(own_parts)
+    far = [pltpu.with_memory_space_constraint(array, pltpu.HBM) for array in (own_gain, own_weight)]
+    on_chip = pl.BlockSpec(memory_space=pltpu.VMEM)
+    in_place = pl.BlockSpec(memory_space=pl.ANY)
+    return pl.pallas_call(
+        functools.partial(attend_kernel, block_rows=block_rows),
+        out_shape=jax.ShapeDtypeStruct((query.shape[0], own_weight.shape[1]), jnp.bfloat16),
+        in_specs=[pl.BlockSpec(memory_space=pltpu.SMEM)] + [on_chip] * 7 + [in_place] * 2,
+        out_specs=on_chip,
+        scratch_shapes=[
+            pltpu.VMEM(own_gain.shape, jnp.float32),
+            pltpu.VMEM(own_weight.shape, jnp.bfloat16),
+            pltpu.SemaphoreType.DMA((2,)),
         ],
-        axis=1,
-    )
-    return jnp.concatenate([rows, tail], axis=1)
+        compiler_params=pltpu.CompilerParams(vmem_limit_bytes=12 * 1024 * 1024),
+        name="attend",
+    )(
+        core.reshape(1).astype(jnp.int32),
+        query,
+        kept(other_parts),
+        own_parts,
+        other_parts,
+        other_gain,
+        other_weight,
+        entering,
+        *far,
+    )
+
+
+def norm_kernel(parts, stream, gain, tail, residual, packed):
+    width = stream.shape[1]
+    total = stream[...].astype(jnp.float32) + jnp.sum(parts[...].astype(jnp.float32), axis=0)
+    residual[...] = total
+    rows = rms_scale(total, gain[...]).astype(packed.dtype)
+    for copy in range(packed.shape[0]):
+        packed[copy, :, :width] = rows
+        packed[copy, :, width:] = tail[...]
+
+
+def normed_copies(parts, stream, gain, tail, copies):
+    rows, width = stream.shape
+    on_chip = pl.BlockSpec(memory_space=pltpu.VMEM)
+    return pl.pallas_call(
+        norm_kernel,
+        out_shape=(
+            jax.ShapeDtypeStruct((rows, width), jnp.float32),
+            jax.ShapeDtypeStruct((copies, rows, width + tail.shape[1]), jnp.bfloat16),
+        ),
+        in_specs=[on_chip] * 4,
+        out_specs=(on_chip, on_chip),
+        compiler_params=pltpu.CompilerParams(vmem_limit_bytes=8 * 1024 * 1024),
+        name="norm",
+    )(parts, stream, gain.reshape(1, -1), tail)
 
 
 def slot_kernel(first, packed, slots, high, low, *, block_rows, top):
@@ -192,7 +285,6 @@
     w_up,
     w_down,
 ):
-    length, head_width = query_rows.shape
     block_rows, model_width = stream.shape
     heads = lax.axis_size("head")
     core = lax.axis_index("pair")
@@ -201,35 +293,25 @@
         "tz,td->zd", all_head_keys, value_rows, preferred_element_type=jnp.float32
     )
     other_gate = lax.ppermute(w_gate, "pair", SWAP)
-    previous, other_gate = lax.optimization_barrier((entering_state(local_state), other_gate))
-    causal = jnp.arange(length)[:, None] >= jnp.arange(length)[None, :]
-    scores = jnp.where(
-        causal,
-        jnp.einsum("tk,sk->ts", query_rows, all_head_keys, preferred_element_type=jnp.float32),
-        0.0,
-    )
-    mixed = jnp.dot(scores, value_rows.astype(jnp.float32))
-    mixed = mixed + jnp.dot(query_rows, previous, preferred_element_type=jnp.float32)
-    attn_normed = rms_scale(mixed, attn_gain[None, :]).astype(jnp.bfloat16)
-
-    by_core = attn_normed.reshape(heads, 2, block_rows, head_width)
-    kept = jnp.where(core == 0, by_core[:, 0], by_core[:, 1]).reshape(-1, head_width)
-    given = jnp.where(core == 0, by_core[:, 1], by_core[:, 0]).reshape(-1, head_width)
-    taken = lax.ppermute(given, "pair", SWAP)
-    partial_rows = jnp.dot(kept, out_weight, preferred_element_type=jnp.float32) + jnp.dot(
-        taken, other_weight, preferred_element_type=jnp.float32
-    )
-    partial_rows = partial_rows.astype(jnp.bfloat16).reshape(heads, block_rows, model_width)
+    own_parts = jnp.stack([query_rows, all_head_keys, value_rows])
+    other_parts = lax.ppermute(own_parts, "pair", SWAP)
+    other_gain = lax.ppermute(attn_gain.reshape(1, -1), "pair", SWAP)
+    previous = entering_state(local_state)
+    partial_rows = attended(
+        core,
+        (own_parts, attn_gain.reshape(1, -1), out_weight),
+        (other_parts, other_gain, other_weight),
+        previous,
+        block_rows,
+    ).reshape(heads, block_rows, model_width)
     other_up = lax.ppermute(w_up, "pair", SWAP)
     other_down = lax.ppermute(w_down, "pair", SWAP)
     partial_rows = lax.all_to_all(partial_rows, "head", 0, 0, tiled=True)
-    projected = jnp.sum(partial_rows.astype(jnp.float32), axis=0)
-    residual = stream.astype(jnp.float32) + projected
-    moe_input = rms_scale(residual, moe_gain).astype(jnp.bfloat16)
-
     my_routes = lax.dynamic_slice_in_dim(routes, core * block_rows, block_rows, 0)
     my_weights = lax.dynamic_slice_in_dim(gate_weights, core * block_rows, block_rows, 0)
-    packed = copied(with_routing(moe_input, my_routes, my_weights), "zh")
+    residual, packed = normed_copies(
+        partial_rows, stream, moe_gain, routing_tail(my_routes, my_weights), lax.axis_size("zh")
+    )
     packed = lax.all_to_all(packed, "zh", 0, 0, tiled=True)
     blocks = packed.shape[0]
     packed = packed.reshape(blocks * block_rows, -1)
@@ -238,7 +320,9 @@
         packed, lax.axis_index("zh") * near, near, block_rows, routes.shape[1]
     )
     slots = slots.reshape(near, -1, model_width)
-    slots, other_up, other_down = lax.optimization_barrier((slots, other_up, other_down))
+    slots, other_gate, other_up, other_down = lax.optimization_barrier(
+        (slots, other_gate, other_up, other_down)
+    )
     rows = lax.all_to_all(slots, NEAR, 0, 0, tiled=True).reshape(-1, model_width)
 
     expert_out = expert(

time: 179 us -> 176 us (0.983)
  blocking collectives: 83.6 us -> 67.3 us
  starting transfers between devices: 40.7 us -> 55.5 us
  matrix products: 6.06 us -> 2.21 us
  Pallas kernels: 6.17 us -> 9.35 us
  waiting for transfers between devices: 34 us -> 36.1 us
    all_to_all x1 -> x0, blocking collectives: 17.7 us -> none  [entering_state(): parts = lax.all_to_all(parts, 'x', 0, 0, tiled=True)]
    ppermute x1 -> x2, starting transfers between devices: 6.79 us -> 17.4 us  [the longest x1 14.7 us: layer(): other_gain = lax.ppermute(attn_gain.reshape(1, -1), 'pair', SWAP)]
    all_to_all x1 -> x2, starting transfers between devices: 5.02 us -> 12 us  [the longest x1 7.77 us: entering_state(): back = lax.all_to_all(entering, ('x', 'pair'), 0, 0, tiled=True)]
    dot_general x4 -> x0, matrix products: 4.5 us -> none  [the longest x1 1.96 us: layer(): jnp.dot(taken, other_weight, preferred_element_type=jnp.float32)]
    pallas_call x0 -> x2, Pallas kernels: none -> 3.18 us  [the longest x1 2.3 us: attended(): pl.pallas_call(functools.partial(attend_kernel, block_rows=block_rows), o...]
  transfers between devices with their start and end apart: 9 -> 11, of which waited for: 4 -> 5; matrix products, arithmetic and copies ran while one was open for 7% -> 2% of each run, Pallas kernels for 0% -> 2%
where the time goes in v5:
time: 176 us; the launch traced here: 175 us
  blocking collectives  67.3 us (38%)
  starting transfers between devices  55.5 us (32%)
  waiting for transfers between devices  36.1 us (21%)
  Pallas kernels  9.35 us (5%)
  other arithmetic  2.44 us (1%)
  matrix products  2.21 us (1%)
    all_to_all x1, blocking collectives, layer(): lax.all_to_all(slots, NEAR, 0, 0, tiled=True).reshape(-1, model_width)  24.2 us
    all_to_all x1, blocking collectives, layer(): sums = lax.all_to_all(sums, 'zh', 0, 0, tiled=True)  24 us
    all_to_all x1, blocking collectives, layer(): returned = lax.all_to_all(expert_out, NEAR, 0, 0, tiled=True)  19.1 us
    all_to_all x1, waiting for transfers between devices, layer(): packed = lax.all_to_all(packed, 'zh', 0, 0, tiled=True)  17.6 us
    ppermute x1, starting transfers between devices, layer(): other_gain = lax.ppermute(attn_gain.reshape(1, -1), 'pair', SWAP)  14.7 us
    all_to_all x1, waiting for transfers between devices, layer(): partial_rows = lax.all_to_all(partial_rows, 'head', 0, 0, tiled=True)  9.94 us
    all_to_all x1, starting transfers between devices, entering_state(): back = lax.all_to_all(entering, ('x', 'pair'), 0, 0, tiled=True)  7.77 us
    all_to_all x1, starting transfers between devices, entering_state(): totals = lax.all_to_all(copies, Z, 0, 0, tiled=True).astype(jnp.float32)  7.02 us
  transfers between devices with their start and end apart: 11, of which 5 were waited for; matrix products, arithmetic and copies ran while one was open for 2% of the time, Pallas kernels for 2%

profile of v5, /device:TPU:7, one launch (start us, length us, event | category | flops | bytes accessed | tf_op | source)
XLA Modules:
  0.0 174.8 jit_solution(1429572211830720516)
XLA Ops:
  0.0 0.0 copy-start
  0.0 0.0 copy-start.1
  0.0 1.6 convolution_convert_fusion
  1.6 4.2 %all-to-all-start = ((bf16[4,32,128]{2,1,0:T(8,128)(2,1)}), bf16[4,32,128]{2,1,0:T(8,128)(2,1)S(1)}, u32[]{:S(2)}, u32[]{:S(2)}) async-start(bf16[4,32,128]{2,1,0:T(8,128)(2,1)} %bitcast.9), calls=%async_computation | async-start | bytes 65536 | tf_op jit(solution)/shard_map/all_to_all | solution.py:37
  5.8 14.7 %collective-permute-start.1 = (f32[1,128]{1,0:T(1,128)}, f32[1,128]{1,0:T(1,128)S(1)}, u32[]{:S(2)}, u32[]{:S(2)}) collective-permute-start(f32[1,128]{1,0:T(1,128)} %bitcast.58), channel_id=1, source_target_pairs={{0,1},{1,0},{2,3},{3,2},{4,5},{5,4},{6,7},{7,6},{8,9},{9,8},{10,11... | collective-permute-start | bytes 1544 | tf_op jit(solution)/shard_map/ppermute | solution.py:298
  20.6 1.9 %collective-permute-start.3 = (bf16[2,2048,384]{2,1,0:T(8,128)(2,1)}, bf16[2,2048,384]{2,1,0:T(8,128)(2,1)}, u32[]{:S(2)}, u32[]{:S(2)}) collective-permute-start(bf16[2,2048,384]{2,1,0:T(8,128)(2,1)} %g0.1), channel_id=1, source_target_pairs={{0,1},{1,0},{2,3},{3,2},{4,5},{5,4},{6,7},{7,6},{8,9},{9,8},{10,11... | collective-permute-start | bytes 9437192 | tf_op jit(solution)/shard_map/ppermute | solution.py:295
  22.5 2.4 %collective-permute-start.4 = (bf16[2,2048,384]{2,1,0:T(8,128)(2,1)}, bf16[2,2048,384]{2,1,0:T(8,128)(2,1)}, u32[]{:S(2)}, u32[]{:S(2)}) collective-permute-start(bf16[2,2048,384]{2,1,0:T(8,128)(2,1)} %u0.1), channel_id=1, source_target_pairs={{0,1},{1,0},{2,3},{3,2},{4,5},{5,4},{6,7},{7,6},{8,9},{9,8},{10,11... | collective-permute-start | bytes 9437192 | tf_op jit(solution)/shard_map/ppermute | solution.py:307
  24.9 1.9 %collective-permute-start.5 = (bf16[2,384,2048]{2,1,0:T(8,128)(2,1)}, bf16[2,384,2048]{2,1,0:T(8,128)(2,1)}, u32[]{:S(2)}, u32[]{:S(2)}) collective-permute-start(bf16[2,384,2048]{2,1,0:T(8,128)(2,1)} %d0.1), channel_id=1, source_target_pairs={{0,1},{1,0},{2,3},{3,2},{4,5},{5,4},{6,7},{7,6},{8,9},{9,8},{10,11... | collective-permute-start | bytes 9437192 | tf_op jit(solution)/shard_map/ppermute | solution.py:308
  26.8 0.0 all-to-all-done
  26.9 0.7 broadcast_in_dim.26
  27.5 7.0 %all-to-all-start.1 = ((bf16[16,32,128]{2,1,0:T(8,128)(2,1)}), bf16[16,32,128]{2,1,0:T(8,128)(2,1)S(1)}, u32[]{:S(2)}, u32[]{:S(2)}) async-start(bf16[16,32,128]{2,1,0:T(8,128)(2,1)} %broadcast_in_dim.26), calls=%async_computation.1 | async-start | bytes 262144 | tf_op jit(solution)/shard_map/all_to_all | solution.py:40
  34.6 0.8 pad_maximum_fusion.parts0
  35.4 2.7 %collective-permute-start = (bf16[3,128,128]{2,1,0:T(8,128)(2,1)S(1)}, bf16[3,128,128]{2,1,0:T(8,128)(2,1)S(1)}, u32[]{:S(2)}, u32[]{:S(2)}) collective-permute-start(bf16[3,128,128]{2,1,0:T(8,128)(2,1)S(1)} %pad_maximum_fusion.parts0), channel_id=1, source_target_pairs={{0,1},{1,0},{2,3},{3,2},{4,5},{5,4},{6,7},{7,6},{8,9},{9,8},{10,11... | collective-permute-start | bytes 294920 | tf_op jit(solution)/shard_map/ppermute | solution.py:297
  38.1 0.0 copy-done
  38.1 0.1 constant_dynamic-slice_fusion.1
  38.2 0.7 fusion.4.q0
  38.9 0.1 collective-permute-done.parts1
  39.0 2.3 %collective-permute-start.2 = (bf16[128,2048]{1,0:T(8,128)(2,1)}, bf16[128,2048]{1,0:T(8,128)(2,1)S(1)}, u32[]{:S(2)}, u32[]{:S(2)}) collective-permute-start(bf16[128,2048]{1,0:T(8,128)(2,1)} %w_in.1), channel_id=1, source_target_pairs={{0,1},{1,0},{2,3},{3,2},{4,5},{5,4},{6,7},{7,6},{8,9},{9,8},{10,11... | collective-permute-start | bytes 1572872 | tf_op jit(solution)/shard_map/ppermute | solution.py:291
  41.3 5.3 %all-to-all-done.1 = bf16[16,32,128]{2,1,0:T(8,128)(2,1)S(1)} async-done(((bf16[16,32,128]{2,1,0:T(8,128)(2,1)}), bf16[16,32,128]{2,1,0:T(8,128)(2,1)S(1)}, u32[]{:S(2)}, u32[]{:S(2)}) %all-to-all-start.1) | async-done | bytes 131104 | tf_op jit(solution)/shard_map/all_to_all | solution.py:40
  46.6 0.1 select_reduce_fusion
  46.7 0.6 broadcast_in_dim.28
  47.3 7.8 %all-to-all-start.2 = ((bf16[8,32,128]{2,1,0:T(8,128)(2,1)}), bf16[8,32,128]{2,1,0:T(8,128)(2,1)S(1)}, u32[]{:S(2)}, u32[]{:S(2)}) async-start(bf16[8,32,128]{2,1,0:T(8,128)(2,1)} %bitcast.11), calls=%async_computation.2 | async-start | bytes 131072 | tf_op jit(solution)/shard_map/all_to_all | solution.py:48
  55.1 3.2 %all-to-all-done.2 = bf16[8,32,128]{2,1,0:T(8,128)(2,1)S(1)} async-done(((bf16[8,32,128]{2,1,0:T(8,128)(2,1)}), bf16[8,32,128]{2,1,0:T(8,128)(2,1)S(1)}, u32[]{:S(2)}, u32[]{:S(2)}) %all-to-all-start.2) | async-done | bytes 65568 | tf_op jit(solution)/shard_map/all_to_all | solution.py:48
  58.3 0.0 collective-permute-done.1.gain1
  58.3 0.0 collective-permute-done.2.w1
  58.3 2.3 %attend.1 = bf16[64,2048]{1,0:T(8,128)(2,1)} custom-call(s32[1]{0:T(128)} %bitcast.core, bf16[64,128]{1,0:T(8,128)(2,1)S(1)} %fusion.4.q0, bf16[64,128]{1,0:T(8,128)(2,1)S(1)} %fusion.3.q1, bf16[3,128,128]{2,1,0:T(8,128)(2,1)S(1)} %pad_maximum_fusion.parts0, bf16[3,128,128]{2,1,0:T(8,128)(2,1)S(1)} %collective-permute-done.parts1, ...), custom_call_target="tpu_custom_call" | custom-call | tf_op jit(solution)/shard_map/attend/pallas_call | solution.py:113
  60.6 6.8 %all-to-all-start.3 = ((bf16[8,8,2048]{2,1,0:T(8,128)(2,1)}), bf16[8,8,2048]{2,1,0:T(8,128)(2,1)S(1)}, u32[]{:S(2)}, u32[]{:S(2)}) async-start(bf16[8,8,2048]{2,1,0:T(8,128)(2,1)} %bitcast.15), calls=%async_computation.3 | async-start | bytes 524288 | tf_op jit(solution)/shard_map/all_to_all | solution.py:309
  67.5 0.0 copy-done.3
  67.5 0.1 constant_dynamic-slice_fusion
  67.5 0.1 copy.21
  67.6 0.1 copy.22
  67.7 0.1 pad.3.clone
  67.8 0.1 maximum_maximum_fusion.tail
  67.9 9.9 %all-to-all-done.3.parts = bf16[8,8,2048]{2,1,0:T(8,128)(2,1)S(1)} async-done(((bf16[8,8,2048]{2,1,0:T(8,128)(2,1)}), bf16[8,8,2048]{2,1,0:T(8,128)(2,1)S(1)}, u32[]{:S(2)}, u32[]{:S(2)}) %all-to-all-start.3) | async-done | bytes 262176 | tf_op jit(solution)/shard_map/all_to_all | solution.py:309
  77.8 0.9 norm.1
  78.7 3.7 %all-to-all-start.4 = ((bf16[8,8,2176]{2,1,0:T(8,128)(2,1)}), bf16[8,8,2176]{2,1,0:T(8,128)(2,1)S(1)}, u32[]{:S(2)}, u32[]{:S(2)}) async-start(bf16[8,8,2176]{2,1,0:T(8,128)(2,1)} %get-tuple-element.15), calls=%async_computation.4 | async-start | bytes 557056 | tf_op jit(solution)/shard_map/all_to_all | solution.py:315
  82.4 17.6 %all-to-all-done.4 = bf16[8,8,2176]{2,1,0:T(8,128)(2,1)S(1)} async-done(((bf16[8,8,2176]{2,1,0:T(8,128)(2,1)}), bf16[8,8,2176]{2,1,0:T(8,128)(2,1)S(1)}, u32[]{:S(2)}, u32[]{:S(2)}) %all-to-all-start.4) | async-done | bytes 278560 | tf_op jit(solution)/shard_map/all_to_all | solution.py:315
  100.1 0.8 slots.1
  100.8 0.0 collective-permute-done.3.g1
  100.8 0.0 collective-permute-done.4.u1
  100.8 0.0 collective-permute-done.5.d1
  100.9 24.2 %all_to_all.40 = bf16[16,16,2048]{2,1,0:T(8,128)(2,1)S(1)} all-to-all(bf16[16,16,2048]{2,1,0:T(8,128)(2,1)S(1)} %bitcast.47), channel_id=1, replica_groups=mesh['zh'=8,'zl'=2,'x'=4,'head'=8,'pair'=2] {'zl','x','pair'}, dimensions={0} | all-to-all | bytes 2097152 | tf_op jit(solution)/shard_map/all_to_all | solution.py:326
  125.1 5.4 %expert.1 = bf16[256,2048]{1,0:T(8,128)(2,1)S(1)} custom-call(s32[1]{0:T(128)} %bitcast.core, bf16[256,2048]{1,0:T(8,128)(2,1)S(1)} %bitcast.44, bf16[2,2048,384]{2,1,0:T(8,128)(2,1)} %g0.1, bf16[2,2048,384]{2,1,0:T(8,128)(2,1)} %u0.1, bf16[2,384,2048]{2,1,0:T(8,128)(2,1)} %d0.1, bf16[2,2048,384]{2,1,0:T(8,128)(2,1)} %collective-permute-done.3.g1, ...), custom_call_target="tpu_custom_call" | custom-call | tf_op jit(solution)/shard_map/expert/pallas_call | solution.py:254
  130.5 19.1 %all_to_all.41 = bf16[16,16,2048]{2,1,0:T(8,128)(2,1)S(1)} all-to-all(bf16[16,16,2048]{2,1,0:T(8,128)(2,1)S(1)} %bitcast.45), channel_id=1, replica_groups=mesh['zh'=8,'zl'=2,'x'=4,'head'=8,'pair'=2] {'zl','x','pair'}, dimensions={0} | all-to-all | bytes 2097152 | tf_op jit(solution)/shard_map/all_to_all | solution.py:331
  149.6 0.3 fusion.9
  149.9 0.3 fusion.1
  150.2 24.0 %all_to_all.42 = bf16[8,8,2048]{2,1,0:T(8,128)(2,1)S(1)} all-to-all(bf16[8,8,2048]{2,1,0:T(8,128)(2,1)S(1)} %fusion.1), channel_id=1, replica_groups=mesh['zh'=8,'zl'=2,'x'=4,'head'=8,'pair'=2] {'zh'}, dimensions={0} | all-to-all | bytes 524288 | tf_op jit(solution)/shard_map/all_to_all | solution.py:337
  174.2 0.6 add_convert_fusion
  (16 shorter events, 0.1 us)
Async XLA Ops:
  0.0 38.1 %copy-start = (s32[16,8]{0,1:T(8,128)S(1)}, s32[16,8]{0,1:T(8,128)}, u32[]{:S(2)}) copy-start(s32[16,8]{0,1:T(8,128)} %param.19) | copy-start | bytes 1540
  0.0 67.5 %copy-start.3 = (f32[16,8]{0,1:T(8,128)S(1)}, f32[16,8]{0,1:T(8,128)}, u32[]{:S(2)}) copy-start(f32[16,8]{0,1:T(8,128)} %param.20) | copy-start | bytes 1540
  0.0 77.8 %copy-start.2 = (f32[2048]{0:T(1024)S(1)}, f32[2048]{0:T(1024)}, u32[]{:S(2)}) copy-start(f32[2048]{0:T(1024)} %param.18) | copy-start | bytes 24580
  0.0 77.8 %copy-start.1 = (bf16[8,2048]{1,0:T(8,128)(2,1)S(1)}, bf16[8,2048]{1,0:T(8,128)(2,1)}, u32[]{:S(2)}) copy-start(bf16[8,2048]{1,0:T(8,128)(2,1)} %stream.1) | copy-start | bytes 98308
  1.6 25.2 %all-to-all-start = ((bf16[4,32,128]{2,1,0:T(8,128)(2,1)}), bf16[4,32,128]{2,1,0:T(8,128)(2,1)S(1)}, u32[]{:S(2)}, u32[]{:S(2)}) async-start(bf16[4,32,128]{2,1,0:T(8,128)(2,1)} %bitcast.9), calls=%async_computation | async-start | bytes 65536 | tf_op jit(solution)/shard_map/all_to_all | solution.py:37
  5.8 52.5 %collective-permute-start.1 = (f32[1,128]{1,0:T(1,128)}, f32[1,128]{1,0:T(1,128)S(1)}, u32[]{:S(2)}, u32[]{:S(2)}) collective-permute-start(f32[1,128]{1,0:T(1,128)} %bitcast.58), channel_id=1, source_target_pairs={{0,1},{1,0},{2,3},{3,2},{4,5},{5,4},{6,7},{7,6},{8,9},{9,8},{10,11... | collective-permute-start | bytes 1544 | tf_op jit(solution)/shard_map/ppermute | solution.py:298
  20.6 80.3 %collective-permute-start.3 = (bf16[2,2048,384]{2,1,0:T(8,128)(2,1)}, bf16[2,2048,384]{2,1,0:T(8,128)(2,1)}, u32[]{:S(2)}, u32[]{:S(2)}) collective-permute-start(bf16[2,2048,384]{2,1,0:T(8,128)(2,1)} %g0.1), channel_id=1, source_target_pairs={{0,1},{1,0},{2,3},{3,2},{4,5},{5,4},{6,7},{7,6},{8,9},{9,8},{10,11... | collective-permute-start | bytes 9437192 | tf_op jit(solution)/shard_map/ppermute | solution.py:295
  22.5 78.3 %collective-permute-start.4 = (bf16[2,2048,384]{2,1,0:T(8,128)(2,1)}, bf16[2,2048,384]{2,1,0:T(8,128)(2,1)}, u32[]{:S(2)}, u32[]{:S(2)}) collective-permute-start(bf16[2,2048,384]{2,1,0:T(8,128)(2,1)} %u0.1), channel_id=1, source_target_pairs={{0,1},{1,0},{2,3},{3,2},{4,5},{5,4},{6,7},{7,6},{8,9},{9,8},{10,11... | collective-permute-start | bytes 9437192 | tf_op jit(solution)/shard_map/ppermute | solution.py:307
  24.9 75.9 %collective-permute-start.5 = (bf16[2,384,2048]{2,1,0:T(8,128)(2,1)}, bf16[2,384,2048]{2,1,0:T(8,128)(2,1)}, u32[]{:S(2)}, u32[]{:S(2)}) collective-permute-start(bf16[2,384,2048]{2,1,0:T(8,128)(2,1)} %d0.1), channel_id=1, source_target_pairs={{0,1},{1,0},{2,3},{3,2},{4,5},{5,4},{6,7},{7,6},{8,9},{9,8},{10,11... | collective-permute-start | bytes 9437192 | tf_op jit(solution)/shard_map/ppermute | solution.py:308
  27.5 19.0 %all-to-all-start.1 = ((bf16[16,32,128]{2,1,0:T(8,128)(2,1)}), bf16[16,32,128]{2,1,0:T(8,128)(2,1)S(1)}, u32[]{:S(2)}, u32[]{:S(2)}) async-start(bf16[16,32,128]{2,1,0:T(8,128)(2,1)} %broadcast_in_dim.26), calls=%async_computation.1 | async-start | bytes 262144 | tf_op jit(solution)/shard_map/all_to_all | solution.py:40
  35.4 3.6 %collective-permute-start = (bf16[3,128,128]{2,1,0:T(8,128)(2,1)S(1)}, bf16[3,128,128]{2,1,0:T(8,128)(2,1)S(1)}, u32[]{:S(2)}, u32[]{:S(2)}) collective-permute-start(bf16[3,128,128]{2,1,0:T(8,128)(2,1)S(1)} %pad_maximum_fusion.parts0), channel_id=1, source_target_pairs={{0,1},{1,0},{2,3},{3,2},{4,5},{5,4},{6,7},{7,6},{8,9},{9,8},{10,11... | collective-permute-start | bytes 294920 | tf_op jit(solution)/shard_map/ppermute | solution.py:297
  39.0 19.3 %collective-permute-start.2 = (bf16[128,2048]{1,0:T(8,128)(2,1)}, bf16[128,2048]{1,0:T(8,128)(2,1)S(1)}, u32[]{:S(2)}, u32[]{:S(2)}) collective-permute-start(bf16[128,2048]{1,0:T(8,128)(2,1)} %w_in.1), channel_id=1, source_target_pairs={{0,1},{1,0},{2,3},{3,2},{4,5},{5,4},{6,7},{7,6},{8,9},{9,8},{10,11... | collective-permute-start | bytes 1572872 | tf_op jit(solution)/shard_map/ppermute | solution.py:291
  47.3 10.9 %all-to-all-start.2 = ((bf16[8,32,128]{2,1,0:T(8,128)(2,1)}), bf16[8,32,128]{2,1,0:T(8,128)(2,1)S(1)}, u32[]{:S(2)}, u32[]{:S(2)}) async-start(bf16[8,32,128]{2,1,0:T(8,128)(2,1)} %bitcast.11), calls=%async_computation.2 | async-start | bytes 131072 | tf_op jit(solution)/shard_map/all_to_all | solution.py:48
  60.6 17.2 %all-to-all-start.3 = ((bf16[8,8,2048]{2,1,0:T(8,128)(2,1)}), bf16[8,8,2048]{2,1,0:T(8,128)(2,1)S(1)}, u32[]{:S(2)}, u32[]{:S(2)}) async-start(bf16[8,8,2048]{2,1,0:T(8,128)(2,1)} %bitcast.15), calls=%async_computation.3 | async-start | bytes 524288 | tf_op jit(solution)/shard_map/all_to_all | solution.py:309
  78.7 21.4 %all-to-all-start.4 = ((bf16[8,8,2176]{2,1,0:T(8,128)(2,1)}), bf16[8,8,2176]{2,1,0:T(8,128)(2,1)S(1)}, u32[]{:S(2)}, u32[]{:S(2)}) async-start(bf16[8,8,2176]{2,1,0:T(8,128)(2,1)} %get-tuple-element.15), calls=%async_computation.4 | async-start | bytes 557056 | tf_op jit(solution)/shard_map/all_to_all | solution.py:315

commit v6 on v5

--- a/solution.py
+++ b/solution.py
@@ -62,8 +62,24 @@
     return jnp.concatenate([expert_ids.astype(jnp.bfloat16), high, low, unused], axis=1)
 
 
+def in_block_kernel(core, q0, q1, parts0, parts1, mixed, *, block_rows):
+    count, length = q0.shape[0], parts0.shape[1]
+    place = lax.broadcasted_iota(jnp.int32, (count, length), 0)
+    row = place // block_rows * 2 * block_rows + core[0] * block_rows + place % block_rows
+    causal = lax.broadcasted_iota(jnp.int32, (count, length), 1) <= row
+    for index, (q, parts) in enumerate(((q0, parts0), (q1, parts1))):
+        scores = lax.dot_general(
+            q[...], parts[1], (((1,), (1,)), ((), ())), preferred_element_type=jnp.float32
+        )
+        scores = jnp.where(causal, scores, 0.0)
+        high = scores.astype(jnp.bfloat16)
+        low = (scores - high.astype(jnp.float32)).astype(jnp.bfloat16)
+        total = jnp.dot(high, parts[2], preferred_element_type=jnp.float32)
+        mixed[index] = total + jnp.dot(low, parts[2], preferred_element_type=jnp.float32)
+
+
 def attend_kernel(
-    core, q0, q1, parts0, parts1, gain1, w1, entering, gain_in, w_in, out, gain0, w0, sems, *, block_rows
+    core, q0, q1, mixed, gain1, w1, entering, gain_in, w_in, out, gain0, w0, sems
 ):
     copies = [
         pltpu.make_async_copy(gain_in, gain0, sems.at[0]),
@@ -72,25 +88,13 @@
     for copy in copies:
         copy.start()
     mine = core[0]
-    count, length = q0.shape[0], parts0.shape[1]
-    place = lax.broadcasted_iota(jnp.int32, (count, length), 0)
-    row = place // block_rows * 2 * block_rows + mine * block_rows + place % block_rows
-    causal = lax.broadcasted_iota(jnp.int32, (count, length), 1) <= row
-
-    def scaled(q, parts, state):
-        scores = lax.dot_general(
-            q[...], parts[1], (((1,), (1,)), ((), ())), preferred_element_type=jnp.float32
-        )
-        scores = jnp.where(causal, scores, 0.0)
-        high = scores.astype(jnp.bfloat16)
-        low = (scores - high.astype(jnp.float32)).astype(jnp.bfloat16)
-        mixed = jnp.dot(high, parts[2], preferred_element_type=jnp.float32)
-        mixed = mixed + jnp.dot(low, parts[2], preferred_element_type=jnp.float32)
-        mixed = mixed + jnp.dot(q[...], state, preferred_element_type=jnp.float32)
-        return rms_scale(mixed, jnp.ones_like(gain1[...]))
-
-    rows1 = (scaled(q1, parts1, entering[1 - mine]) * gain1[...]).astype(jnp.bfloat16)
-    rows0 = scaled(q0, parts0, entering[mine])
+
+    def scaled(q, index, state):
+        total = mixed[index] + jnp.dot(q[...], state, preferred_element_type=jnp.float32)
+        return rms_scale(total, jnp.ones_like(gain1[...]))
+
+    rows1 = (scaled(q1, 1, entering[1 - mine]) * gain1[...]).astype(jnp.bfloat16)
+    rows0 = scaled(q0, 0, entering[mine])
     for copy in copies:
         copy.wait()
     rows0 = (rows0 * gain0[...]).astype(jnp.bfloat16)
@@ -99,21 +103,33 @@
     out[...] = total.astype(out.dtype)
 
 
-def attended(core, own, other, entering, block_rows):
+def in_block(core, own_parts, other_parts, block_rows):
     def kept(parts):
         by_core = parts[0].reshape(-1, 2, block_rows, parts.shape[2])
         return jnp.where(core == 0, by_core[:, 0], by_core[:, 1]).reshape(-1, parts.shape[2])
 
-    own_parts, own_gain, own_weight = own
-    other_parts, other_gain, other_weight = other
-    query = kept(own_parts)
-    far = [pltpu.with_memory_space_constraint(array, pltpu.HBM) for array in (own_gain, own_weight)]
+    queries = (kept(own_parts), kept(other_parts))
+    on_chip = pl.BlockSpec(memory_space=pltpu.VMEM)
+    mixed = pl.pallas_call(
+        functools.partial(in_block_kernel, block_rows=block_rows),
+        out_shape=jax.ShapeDtypeStruct((2, *queries[0].shape), jnp.float32),
+        in_specs=[pl.BlockSpec(memory_space=pltpu.SMEM)] + [on_chip] * 4,
+        out_specs=on_chip,
+        compiler_params=pltpu.CompilerParams(vmem_limit_bytes=8 * 1024 * 1024),
+        name="in_block",
+    )(core.reshape(1).astype(jnp.int32), *queries, own_parts, other_parts)
+    return queries, mixed
+
+
+def attended(core, queries, mixed, own, other, entering):
+    own_gain, own_weight = own
+    far = [pltpu.with_memory_space_constraint(array, pltpu.HBM) for array in own]
     on_chip = pl.BlockSpec(memory_space=pltpu.VMEM)
     in_place = pl.BlockSpec(memory_space=pl.ANY)
     return pl.pallas_call(
-        functools.partial(attend_kernel, block_rows=block_rows),
-        out_shape=jax.ShapeDtypeStruct((query.shape[0], own_weight.shape[1]), jnp.bfloat16),
-        in_specs=[pl.BlockSpec(memory_space=pltpu.SMEM)] + [on_chip] * 7 + [in_place] * 2,
+        attend_kernel,
+        out_shape=jax.ShapeDtypeStruct((mixed.shape[1], own_weight.shape[1]), jnp.bfloat16),
+        in_specs=[pl.BlockSpec(memory_space=pltpu.SMEM)] + [on_chip] * 6 + [in_place] * 2,
         out_specs=on_chip,
         scratch_shapes=[
             pltpu.VMEM(own_gain.shape, jnp.float32),
@@ -122,17 +138,7 @@
         ],
         compiler_params=pltpu.CompilerParams(vmem_limit_bytes=12 * 1024 * 1024),
         name="attend",
-    )(
-        core.reshape(1).astype(jnp.int32),
-        query,
-        kept(other_parts),
-        own_parts,
-        other_parts,
-        other_gain,
-        other_weight,
-        entering,
-        *far,
-    )
+    )(core.reshape(1).astype(jnp.int32), *queries, mixed, *other, entering, *far)
 
 
 def norm_kernel(parts, stream, gain, tail, residual, packed):
@@ -296,13 +302,15 @@
     own_parts = jnp.stack([query_rows, all_head_keys, value_rows])
     other_parts = lax.ppermute(own_parts, "pair", SWAP)
     other_gain = lax.ppermute(attn_gain.reshape(1, -1), "pair", SWAP)
+    queries, mixed = in_block(core, own_parts, other_parts, block_rows)
     previous = entering_state(local_state)
     partial_rows = attended(
         core,
-        (own_parts, attn_gain.reshape(1, -1), out_weight),
-        (other_parts, other_gain, other_weight),
+        queries,
+        mixed,
+        (attn_gain.reshape(1, -1), out_weight),
+        (other_gain, other_weight),
         previous,
-        block_rows,
     ).reshape(heads, block_rows, model_width)
     other_up = lax.ppermute(w_up, "pair", SWAP)
     other_down = lax.ppermute(w_down, "pair", SWAP)

time: 176 us -> 176 us (level)
  no operation moved by 1% of the time
where the time goes in v6:
time: 176 us; the launch traced here: 175 us
  blocking collectives  67.3 us (38%)
  starting transfers between devices  55.5 us (32%)
  waiting for transfers between devices  35.8 us (20%)
  Pallas kernels  9.47 us (5%)
  other arithmetic  2.44 us (1%)
  matrix products  2.21 us (1%)
    all_to_all x1, blocking collectives, layer(): lax.all_to_all(slots, NEAR, 0, 0, tiled=True).reshape(-1, model_width)  24.2 us
    all_to_all x1, blocking collectives, layer(): sums = lax.all_to_all(sums, 'zh', 0, 0, tiled=True)  24 us
    all_to_all x1, blocking collectives, layer(): returned = lax.all_to_all(expert_out, NEAR, 0, 0, tiled=True)  19.1 us
    all_to_all x1, waiting for transfers between devices, layer(): packed = lax.all_to_all(packed, 'zh', 0, 0, tiled=True)  17.6 us
    ppermute x1, starting transfers between devices, layer(): other_gain = lax.ppermute(attn_gain.reshape(1, -1), 'pair', SWAP)  14.7 us
    all_to_all x1, waiting for transfers between devices, layer(): partial_rows = lax.all_to_all(partial_rows, 'head', 0, 0, tiled=True)  9.95 us
    all_to_all x1, starting transfers between devices, entering_state(): back = lax.all_to_all(entering, ('x', 'pair'), 0, 0, tiled=True)  7.77 us
    all_to_all x1, starting transfers between devices, entering_state(): totals = lax.all_to_all(copies, Z, 0, 0, tiled=True).astype(jnp.float32)  7.02 us
  transfers between devices with their start and end apart: 11, of which 5 were waited for; matrix products, arithmetic and copies ran while one was open for 2% of the time, Pallas kernels for 2%

profile of v6, /device:TPU:7, one launch (start us, length us, event | category | flops | bytes accessed | tf_op | source)
XLA Modules:
  0.0 174.6 jit_solution(12063551763898236186)
XLA Ops:
  0.0 0.0 copy-start
  0.0 0.0 copy-start.1
  0.0 1.6 convolution_convert_fusion
  1.6 4.2 %all-to-all-start = ((bf16[4,32,128]{2,1,0:T(8,128)(2,1)}), bf16[4,32,128]{2,1,0:T(8,128)(2,1)S(1)}, u32[]{:S(2)}, u32[]{:S(2)}) async-start(bf16[4,32,128]{2,1,0:T(8,128)(2,1)} %bitcast.9), calls=%async_computation | async-start | bytes 65536 | tf_op jit(solution)/shard_map/all_to_all | solution.py:37
  5.8 14.7 %collective-permute-start.1 = (f32[1,128]{1,0:T(1,128)}, f32[1,128]{1,0:T(1,128)S(1)}, u32[]{:S(2)}, u32[]{:S(2)}) collective-permute-start(f32[1,128]{1,0:T(1,128)} %bitcast.78), channel_id=1, source_target_pairs={{0,1},{1,0},{2,3},{3,2},{4,5},{5,4},{6,7},{7,6},{8,9},{9,8},{10,11... | collective-permute-start | bytes 1544 | tf_op jit(solution)/shard_map/ppermute | solution.py:304
  20.6 1.9 %collective-permute-start.3 = (bf16[2,2048,384]{2,1,0:T(8,128)(2,1)}, bf16[2,2048,384]{2,1,0:T(8,128)(2,1)}, u32[]{:S(2)}, u32[]{:S(2)}) collective-permute-start(bf16[2,2048,384]{2,1,0:T(8,128)(2,1)} %g0.1), channel_id=1, source_target_pairs={{0,1},{1,0},{2,3},{3,2},{4,5},{5,4},{6,7},{7,6},{8,9},{9,8},{10,11... | collective-permute-start | bytes 9437192 | tf_op jit(solution)/shard_map/ppermute | solution.py:301
  22.5 2.4 %collective-permute-start.4 = (bf16[2,2048,384]{2,1,0:T(8,128)(2,1)}, bf16[2,2048,384]{2,1,0:T(8,128)(2,1)}, u32[]{:S(2)}, u32[]{:S(2)}) collective-permute-start(bf16[2,2048,384]{2,1,0:T(8,128)(2,1)} %u0.1), channel_id=1, source_target_pairs={{0,1},{1,0},{2,3},{3,2},{4,5},{5,4},{6,7},{7,6},{8,9},{9,8},{10,11... | collective-permute-start | bytes 9437192 | tf_op jit(solution)/shard_map/ppermute | solution.py:315
  24.9 1.9 %collective-permute-start.5 = (bf16[2,384,2048]{2,1,0:T(8,128)(2,1)}, bf16[2,384,2048]{2,1,0:T(8,128)(2,1)}, u32[]{:S(2)}, u32[]{:S(2)}) collective-permute-start(bf16[2,384,2048]{2,1,0:T(8,128)(2,1)} %d0.1), channel_id=1, source_target_pairs={{0,1},{1,0},{2,3},{3,2},{4,5},{5,4},{6,7},{7,6},{8,9},{9,8},{10,11... | collective-permute-start | bytes 9437192 | tf_op jit(solution)/shard_map/ppermute | solution.py:316
  26.8 0.0 all-to-all-done
  26.9 0.7 broadcast_in_dim.26
  27.5 7.0 %all-to-all-start.1 = ((bf16[16,32,128]{2,1,0:T(8,128)(2,1)}), bf16[16,32,128]{2,1,0:T(8,128)(2,1)S(1)}, u32[]{:S(2)}, u32[]{:S(2)}) async-start(bf16[16,32,128]{2,1,0:T(8,128)(2,1)} %broadcast_in_dim.26), calls=%async_computation.1 | async-start | bytes 262144 | tf_op jit(solution)/shard_map/all_to_all | solution.py:40
  34.6 0.8 pad_maximum_fusion.parts0
  35.4 2.7 %collective-permute-start = (bf16[3,128,128]{2,1,0:T(8,128)(2,1)S(1)}, bf16[3,128,128]{2,1,0:T(8,128)(2,1)S(1)}, u32[]{:S(2)}, u32[]{:S(2)}) collective-permute-start(bf16[3,128,128]{2,1,0:T(8,128)(2,1)S(1)} %pad_maximum_fusion.parts0), channel_id=1, source_target_pairs={{0,1},{1,0},{2,3},{3,2},{4,5},{5,4},{6,7},{7,6},{8,9},{9,8},{10,11... | collective-permute-start | bytes 294920 | tf_op jit(solution)/shard_map/ppermute | solution.py:303
  38.1 0.0 copy-done
  38.1 0.1 constant_dynamic-slice_fusion.1
  38.2 0.7 fusion.6.q0
  38.9 0.1 collective-permute-done.parts1
  39.0 2.3 %collective-permute-start.2 = (bf16[128,2048]{1,0:T(8,128)(2,1)}, bf16[128,2048]{1,0:T(8,128)(2,1)S(1)}, u32[]{:S(2)}, u32[]{:S(2)}) collective-permute-start(bf16[128,2048]{1,0:T(8,128)(2,1)} %w_in.1), channel_id=1, source_target_pairs={{0,1},{1,0},{2,3},{3,2},{4,5},{5,4},{6,7},{7,6},{8,9},{9,8},{10,11... | collective-permute-start | bytes 1572872 | tf_op jit(solution)/shard_map/ppermute | solution.py:297
  41.3 5.3 %all-to-all-done.1 = bf16[16,32,128]{2,1,0:T(8,128)(2,1)S(1)} async-done(((bf16[16,32,128]{2,1,0:T(8,128)(2,1)}), bf16[16,32,128]{2,1,0:T(8,128)(2,1)S(1)}, u32[]{:S(2)}, u32[]{:S(2)}) %all-to-all-start.1) | async-done | bytes 131104 | tf_op jit(solution)/shard_map/all_to_all | solution.py:40
  46.6 0.1 select_reduce_fusion
  46.7 0.6 broadcast_in_dim.28
  47.3 7.8 %all-to-all-start.2 = ((bf16[8,32,128]{2,1,0:T(8,128)(2,1)}), bf16[8,32,128]{2,1,0:T(8,128)(2,1)S(1)}, u32[]{:S(2)}, u32[]{:S(2)}) async-start(bf16[8,32,128]{2,1,0:T(8,128)(2,1)} %bitcast.11), calls=%async_computation.2 | async-start | bytes 131072 | tf_op jit(solution)/shard_map/all_to_all | solution.py:48
  55.1 0.3 in_block.1.mixed
  55.4 2.8 %all-to-all-done.2 = bf16[8,32,128]{2,1,0:T(8,128)(2,1)S(1)} async-done(((bf16[8,32,128]{2,1,0:T(8,128)(2,1)}), bf16[8,32,128]{2,1,0:T(8,128)(2,1)S(1)}, u32[]{:S(2)}, u32[]{:S(2)}) %all-to-all-start.2) | async-done | bytes 65568 | tf_op jit(solution)/shard_map/all_to_all | solution.py:48
  58.3 0.0 collective-permute-done.1.gain1
  58.3 0.0 collective-permute-done.2.w1
  58.3 2.1 %attend.1 = bf16[64,2048]{1,0:T(8,128)(2,1)} custom-call(s32[1]{0:T(128)} %bitcast.core, bf16[64,128]{1,0:T(8,128)(2,1)S(1)} %fusion.6.q0, bf16[64,128]{1,0:T(8,128)(2,1)S(1)} %fusion.4.q1, f32[2,64,128]{2,1,0:T(8,128)S(1)} %in_block.1.mixed, f32[1,128]{1,0:T(1,128)S(1)} %collective-permute-done.1.gain1, bf16[128,2048]{1,0:T(8,128)(2,1)S(1)} %collective-permute-done.2.w1, ...), custom_call_target="tpu_custom_call" | custom-call | tf_op jit(solution)/shard_map/attend/pallas_call | solution.py:129
  60.4 6.8 %all-to-all-start.3 = ((bf16[8,8,2048]{2,1,0:T(8,128)(2,1)}), bf16[8,8,2048]{2,1,0:T(8,128)(2,1)S(1)}, u32[]{:S(2)}, u32[]{:S(2)}) async-start(bf16[8,8,2048]{2,1,0:T(8,128)(2,1)} %bitcast.15), calls=%async_computation.3 | async-start | bytes 524288 | tf_op jit(solution)/shard_map/all_to_all | solution.py:317
  67.3 0.1 constant_dynamic-slice_fusion
  67.3 0.1 copy.37
  67.4 0.1 copy.38
  67.5 0.1 pad.3.clone
  67.6 0.1 maximum_maximum_fusion.tail
  67.7 9.9 %all-to-all-done.3.parts = bf16[8,8,2048]{2,1,0:T(8,128)(2,1)S(1)} async-done(((bf16[8,8,2048]{2,1,0:T(8,128)(2,1)}), bf16[8,8,2048]{2,1,0:T(8,128)(2,1)S(1)}, u32[]{:S(2)}, u32[]{:S(2)}) %all-to-all-start.3) | async-done | bytes 262176 | tf_op jit(solution)/shard_map/all_to_all | solution.py:317
  77.6 0.9 norm.1
  78.5 3.7 %all-to-all-start.4 = ((bf16[8,8,2176]{2,1,0:T(8,128)(2,1)}), bf16[8,8,2176]{2,1,0:T(8,128)(2,1)S(1)}, u32[]{:S(2)}, u32[]{:S(2)}) async-start(bf16[8,8,2176]{2,1,0:T(8,128)(2,1)} %get-tuple-element.15), calls=%async_computation.4 | async-start | bytes 557056 | tf_op jit(solution)/shard_map/all_to_all | solution.py:323
  82.2 17.6 %all-to-all-done.4 = bf16[8,8,2176]{2,1,0:T(8,128)(2,1)S(1)} async-done(((bf16[8,8,2176]{2,1,0:T(8,128)(2,1)}), bf16[8,8,2176]{2,1,0:T(8,128)(2,1)S(1)}, u32[]{:S(2)}, u32[]{:S(2)}) %all-to-all-start.4) | async-done | bytes 278560 | tf_op jit(solution)/shard_map/all_to_all | solution.py:323
  99.9 0.8 slots.1
  100.6 0.0 collective-permute-done.3.g1
  100.6 0.0 collective-permute-done.4.u1
  100.6 0.0 collective-permute-done.5.d1
  100.7 24.2 %all_to_all.40 = bf16[16,16,2048]{2,1,0:T(8,128)(2,1)S(1)} all-to-all(bf16[16,16,2048]{2,1,0:T(8,128)(2,1)S(1)} %bitcast.67), channel_id=1, replica_groups=mesh['zh'=8,'zl'=2,'x'=4,'head'=8,'pair'=2] {'zl','x','pair'}, dimensions={0} | all-to-all | bytes 2097152 | tf_op jit(solution)/shard_map/all_to_all | solution.py:334
  124.9 5.4 %expert.1 = bf16[256,2048]{1,0:T(8,128)(2,1)S(1)} custom-call(s32[1]{0:T(128)} %bitcast.core, bf16[256,2048]{1,0:T(8,128)(2,1)S(1)} %bitcast.64, bf16[2,2048,384]{2,1,0:T(8,128)(2,1)} %g0.1, bf16[2,2048,384]{2,1,0:T(8,128)(2,1)} %u0.1, bf16[2,384,2048]{2,1,0:T(8,128)(2,1)} %d0.1, bf16[2,2048,384]{2,1,0:T(8,128)(2,1)} %collective-permute-done.3.g1, ...), custom_call_target="tpu_custom_call" | custom-call | tf_op jit(solution)/shard_map/expert/pallas_call | solution.py:260
  130.3 19.1 %all_to_all.41 = bf16[16,16,2048]{2,1,0:T(8,128)(2,1)S(1)} all-to-all(bf16[16,16,2048]{2,1,0:T(8,128)(2,1)S(1)} %bitcast.65), channel_id=1, replica_groups=mesh['zh'=8,'zl'=2,'x'=4,'head'=8,'pair'=2] {'zl','x','pair'}, dimensions={0} | all-to-all | bytes 2097152 | tf_op jit(solution)/shard_map/all_to_all | solution.py:339
  149.4 0.3 fusion.11
  149.7 0.3 fusion.1
  150.0 24.0 %all_to_all.42 = bf16[8,8,2048]{2,1,0:T(8,128)(2,1)S(1)} all-to-all(bf16[8,8,2048]{2,1,0:T(8,128)(2,1)S(1)} %fusion.1), channel_id=1, replica_groups=mesh['zh'=8,'zl'=2,'x'=4,'head'=8,'pair'=2] {'zh'}, dimensions={0} | all-to-all | bytes 524288 | tf_op jit(solution)/shard_map/all_to_all | solution.py:345
  174.0 0.6 add_convert_fusion
  (17 shorter events, 0.1 us)
Async XLA Ops:
  0.0 38.1 %copy-start = (s32[16,8]{0,1:T(8,128)S(1)}, s32[16,8]{0,1:T(8,128)}, u32[]{:S(2)}) copy-start(s32[16,8]{0,1:T(8,128)} %param.19) | copy-start | bytes 1540
  0.0 67.3 %copy-start.3 = (f32[16,8]{0,1:T(8,128)S(1)}, f32[16,8]{0,1:T(8,128)}, u32[]{:S(2)}) copy-start(f32[16,8]{0,1:T(8,128)} %param.20) | copy-start | bytes 1540
  0.0 77.6 %copy-start.2 = (f32[2048]{0:T(1024)S(1)}, f32[2048]{0:T(1024)}, u32[]{:S(2)}) copy-start(f32[2048]{0:T(1024)} %param.18) | copy-start | bytes 24580
  0.0 77.6 %copy-start.1 = (bf16[8,2048]{1,0:T(8,128)(2,1)S(1)}, bf16[8,2048]{1,0:T(8,128)(2,1)}, u32[]{:S(2)}) copy-start(bf16[8,2048]{1,0:T(8,128)(2,1)} %stream.1) | copy-start | bytes 98308
  1.6 25.2 %all-to-all-start = ((bf16[4,32,128]{2,1,0:T(8,128)(2,1)}), bf16[4,32,128]{2,1,0:T(8,128)(2,1)S(1)}, u32[]{:S(2)}, u32[]{:S(2)}) async-start(bf16[4,32,128]{2,1,0:T(8,128)(2,1)} %bitcast.9), calls=%async_computation | async-start | bytes 65536 | tf_op jit(solution)/shard_map/all_to_all | solution.py:37
  5.8 52.5 %collective-permute-start.1 = (f32[1,128]{1,0:T(1,128)}, f32[1,128]{1,0:T(1,128)S(1)}, u32[]{:S(2)}, u32[]{:S(2)}) collective-permute-start(f32[1,128]{1,0:T(1,128)} %bitcast.78), channel_id=1, source_target_pairs={{0,1},{1,0},{2,3},{3,2},{4,5},{5,4},{6,7},{7,6},{8,9},{9,8},{10,11... | collective-permute-start | bytes 1544 | tf_op jit(solution)/shard_map/ppermute | solution.py:304
  20.6 80.1 %collective-permute-start.3 = (bf16[2,2048,384]{2,1,0:T(8,128)(2,1)}, bf16[2,2048,384]{2,1,0:T(8,128)(2,1)}, u32[]{:S(2)}, u32[]{:S(2)}) collective-permute-start(bf16[2,2048,384]{2,1,0:T(8,128)(2,1)} %g0.1), channel_id=1, source_target_pairs={{0,1},{1,0},{2,3},{3,2},{4,5},{5,4},{6,7},{7,6},{8,9},{9,8},{10,11... | collective-permute-start | bytes 9437192 | tf_op jit(solution)/shard_map/ppermute | solution.py:301
  22.5 78.2 %collective-permute-start.4 = (bf16[2,2048,384]{2,1,0:T(8,128)(2,1)}, bf16[2,2048,384]{2,1,0:T(8,128)(2,1)}, u32[]{:S(2)}, u32[]{:S(2)}) collective-permute-start(bf16[2,2048,384]{2,1,0:T(8,128)(2,1)} %u0.1), channel_id=1, source_target_pairs={{0,1},{1,0},{2,3},{3,2},{4,5},{5,4},{6,7},{7,6},{8,9},{9,8},{10,11... | collective-permute-start | bytes 9437192 | tf_op jit(solution)/shard_map/ppermute | solution.py:315
  24.9 75.7 %collective-permute-start.5 = (bf16[2,384,2048]{2,1,0:T(8,128)(2,1)}, bf16[2,384,2048]{2,1,0:T(8,128)(2,1)}, u32[]{:S(2)}, u32[]{:S(2)}) collective-permute-start(bf16[2,384,2048]{2,1,0:T(8,128)(2,1)} %d0.1), channel_id=1, source_target_pairs={{0,1},{1,0},{2,3},{3,2},{4,5},{5,4},{6,7},{7,6},{8,9},{9,8},{10,11... | collective-permute-start | bytes 9437192 | tf_op jit(solution)/shard_map/ppermute | solution.py:316
  27.5 19.0 %all-to-all-start.1 = ((bf16[16,32,128]{2,1,0:T(8,128)(2,1)}), bf16[16,32,128]{2,1,0:T(8,128)(2,1)S(1)}, u32[]{:S(2)}, u32[]{:S(2)}) async-start(bf16[16,32,128]{2,1,0:T(8,128)(2,1)} %broadcast_in_dim.26), calls=%async_computation.1 | async-start | bytes 262144 | tf_op jit(solution)/shard_map/all_to_all | solution.py:40
  35.4 3.6 %collective-permute-start = (bf16[3,128,128]{2,1,0:T(8,128)(2,1)S(1)}, bf16[3,128,128]{2,1,0:T(8,128)(2,1)S(1)}, u32[]{:S(2)}, u32[]{:S(2)}) collective-permute-start(bf16[3,128,128]{2,1,0:T(8,128)(2,1)S(1)} %pad_maximum_fusion.parts0), channel_id=1, source_target_pairs={{0,1},{1,0},{2,3},{3,2},{4,5},{5,4},{6,7},{7,6},{8,9},{9,8},{10,11... | collective-permute-start | bytes 294920 | tf_op jit(solution)/shard_map/ppermute | solution.py:303
  39.0 19.3 %collective-permute-start.2 = (bf16[128,2048]{1,0:T(8,128)(2,1)}, bf16[128,2048]{1,0:T(8,128)(2,1)S(1)}, u32[]{:S(2)}, u32[]{:S(2)}) collective-permute-start(bf16[128,2048]{1,0:T(8,128)(2,1)} %w_in.1), channel_id=1, source_target_pairs={{0,1},{1,0},{2,3},{3,2},{4,5},{5,4},{6,7},{7,6},{8,9},{9,8},{10,11... | collective-permute-start | bytes 1572872 | tf_op jit(solution)/shard_map/ppermute | solution.py:297
  47.3 10.9 %all-to-all-start.2 = ((bf16[8,32,128]{2,1,0:T(8,128)(2,1)}), bf16[8,32,128]{2,1,0:T(8,128)(2,1)S(1)}, u32[]{:S(2)}, u32[]{:S(2)}) async-start(bf16[8,32,128]{2,1,0:T(8,128)(2,1)} %bitcast.11), calls=%async_computation.2 | async-start | bytes 131072 | tf_op jit(solution)/shard_map/all_to_all | solution.py:48
  60.4 17.2 %all-to-all-start.3 = ((bf16[8,8,2048]{2,1,0:T(8,128)(2,1)}), bf16[8,8,2048]{2,1,0:T(8,128)(2,1)S(1)}, u32[]{:S(2)}, u32[]{:S(2)}) async-start(bf16[8,8,2048]{2,1,0:T(8,128)(2,1)} %bitcast.15), calls=%async_computation.3 | async-start | bytes 524288 | tf_op jit(solution)/shard_map/all_to_all | solution.py:317
  78.5 21.4 %all-to-all-start.4 = ((bf16[8,8,2176]{2,1,0:T(8,128)(2,1)}), bf16[8,8,2176]{2,1,0:T(8,128)(2,1)S(1)}, u32[]{:S(2)}, u32[]{:S(2)}) async-start(bf16[8,8,2176]{2,1,0:T(8,128)(2,1)} %get-tuple-element.15), calls=%async_computation.4 | async-start | bytes 557056 | tf_op jit(solution)/shard_map/all_to_all | solution.py:323
